TPU v7x, 512 devices: a whole 4x4x16 slice. The times are simulated.
512 devices in a mesh: hx: 32 (over x, z_lo), hy: 4 (over y), vz: 4 (over z_hi, core).
Axes of the slice: x: 4, y: 4, z: 16 (z_hi: 2, z_lo: 8; z = z_hi * 8 + z_lo), core: 2. Of those that a mesh axis runs over, the one named last changes fastest.
Arguments:
- prognostic: float32 [5, 80, 4, 4, 4, 4096], P(None, 'vz', None, None, 'hy', 'hx'), may hold values from -6 to 6
- metric: float32 [4, 4, 4, 4096], P(None, None, 'hy', 'hx'), may hold values from 0.5 to 2
- first_flux: float32 [5, 5], replicated, may hold values from -2.5 to 2.5
- second_flux: float32 [5, 5], replicated, may hold values from -2.5 to 2.5
- neighbour_face: int32 [4, 4, 4096], P(None, 'hy', 'hx'), may hold values from 0 to 3
- orientation: int32 [4, 4, 4096], P(None, 'hy', 'hx'), may hold values from 0 to 1
- coupling: float32 [4, 80, 4, 4, 4, 4096], P(None, None, 'vz', None, 'hy', 'hx'), may hold values from 0.1 to 1
- damping: float32 [4, 4, 4, 4096], P('vz', None, 'hy', 'hx'), may hold values from 0.005 to 0.05
Outputs:
- updated: float32 [5, 80, 4, 4, 4, 4096], P(None, 'vz', None, None, 'hy', 'hx')
All inputs are finite; a program needn't handle non-finite values.
Results may differ from a plain program's by a relative error of at most 0.0003.
Values sent between devices are 32-bit elements; how exact they have to be, the bound alone decides.
A program may use at most 64 MiB of HBM per device.

v0:
```python
import jax
import jax.numpy as jnp
import numpy as np
from jax import lax
from jax.sharding import PartitionSpec as P

step_size = 0.05
rusanov_speed = 1.0
lift_weight = 6.0
gravity_couple = 0.5
density_couple = 0.3
theta_couple = 0.4


def extended(x, sides, width):
    for axis, dim in sides:
        size, length = (lax.axis_size(axis), x.shape[dim])
        up = [(i, (i + 1) % size) for i in range(size)]
        down = [(j, i) for i, j in up]
        last = lax.slice_in_dim(x, length - width, length, axis=dim)
        initial = lax.slice_in_dim(x, 0, width, axis=dim)
        before = lax.ppermute(last, axis, up)
        after = lax.ppermute(initial, axis, down)
        x = jnp.concatenate([before, x, after], axis=dim)
    return x


def derivative_table():
    points = np.array([-1.0, -1.0 / np.sqrt(5.0), 1.0 / np.sqrt(5.0), 1.0])
    number = points.shape[0]
    barycentric = np.ones(number)
    for source in range(number):
        for another in range(number):
            if another != source:
                barycentric[source] = barycentric[source] / (points[source] - points[another])
    matrix = np.zeros((number, number))
    for target in range(number):
        for source in range(number):
            if target != source:
                matrix[target, source] = (
                    barycentric[source] / barycentric[target] / (points[target] - points[source])
                )
        matrix[target, target] = -np.sum(matrix[target])
    return jnp.asarray(matrix, dtype=jnp.float32)


def face_traces(fields):
    west_face = fields[:, :, :, 0]
    east_face = fields[:, :, :, -1]
    south_face = fields[:, :, 0, :]
    north_face = fields[:, :, -1, :]
    return jnp.stack([west_face, east_face, south_face, north_face], axis=2)


def pick_face(candidates, table_row, flip_row):
    chosen = jnp.zeros(candidates.shape[:2] + candidates.shape[3:], candidates.dtype)
    for option in range(candidates.shape[2]):
        chosen = chosen + jnp.where(table_row == option, candidates[:, :, option], 0.0)
    reverse = chosen[:, :, ::-1]
    return jnp.where(flip_row == 1, reverse, chosen)


def section_values(fields, outer_traces, metric, first_flux, second_flux):
    derivative = derivative_table()
    highest = lax.Precision.HIGHEST
    flux_first = jnp.einsum("fg,gljiab->fljiab", first_flux, fields, precision=highest)
    flux_second = jnp.einsum("fg,gljiab->fljiab", second_flux, fields, precision=highest)
    divergence = jnp.einsum("ci,fljiab->fljcab", derivative, flux_first, precision=highest)
    divergence = divergence + jnp.einsum(
        "cj,fljiab->flciab", derivative, flux_second, precision=highest
    )
    own_traces = face_traces(fields)
    own_first = face_traces(flux_first)
    own_second = face_traces(flux_second)
    own_normal = jnp.stack(
        [-own_first[:, :, 0], own_first[:, :, 1], -own_second[:, :, 2], own_second[:, :, 3]], axis=2
    )
    outer_first = jnp.einsum(
        "fg,glhkab->flhkab", first_flux, outer_traces[:, :, 0:2], precision=highest
    )
    outer_second = jnp.einsum(
        "fg,glhkab->flhkab", second_flux, outer_traces[:, :, 2:4], precision=highest
    )
    outer_normal = jnp.concatenate(
        [
            -outer_first[:, :, 0:1],
            outer_first[:, :, 1:2],
            -outer_second[:, :, 0:1],
            outer_second[:, :, 1:2],
        ],
        axis=2,
    )
    correction = 0.5 * (own_normal - outer_normal) + 0.5 * rusanov_speed * (
        outer_traces - own_traces
    )
    blank_face = jnp.zeros_like(correction[:, :, 0])
    middle_blanks = [blank_face] * (fields.shape[3] - 2)
    across_first = jnp.stack([correction[:, :, 0]] + middle_blanks + [correction[:, :, 1]], axis=3)
    across_second = jnp.stack([correction[:, :, 2]] + middle_blanks + [correction[:, :, 3]], axis=2)
    tendency = metric * (lift_weight * (across_first + across_second) - divergence)
    return fields + step_size * tendency


def level_difference(column_values):
    upper_part = jnp.concatenate([column_values[1:], jnp.zeros_like(column_values[:1])], axis=0)
    lower_part = jnp.concatenate([jnp.zeros_like(column_values[:1]), column_values[:-1]], axis=0)
    return upper_part - lower_part


def solve_unrolled(entry_a, entry_b, centre, entry_d, entry_e, source):
    levels = source.shape[0]
    empty_row = jnp.zeros_like(source[0])
    far_ratio, far_second, far_value = (empty_row, empty_row, empty_row)
    near_ratio, near_second, near_value = (empty_row, empty_row, empty_row)
    ratios, seconds, scaled = ([], [], [])
    for height in range(levels):
        reduced = entry_b[height] - entry_a[height] * far_ratio
        pivot_entry = centre[height] - entry_a[height] * far_second - reduced * near_ratio
        upper_ratio = (entry_d[height] - reduced * near_second) / pivot_entry
        second_ratio = entry_e[height] / pivot_entry
        scaled_value = (
            source[height] - entry_a[height] * far_value - reduced * near_value
        ) / pivot_entry
        far_ratio, far_second, far_value = (near_ratio, near_second, near_value)
        near_ratio, near_second, near_value = (upper_ratio, second_ratio, scaled_value)
        ratios.append(upper_ratio)
        seconds.append(second_ratio)
        scaled.append(scaled_value)
    next_one, next_two = (empty_row, empty_row)
    solution = [None] * levels
    for height in range(levels - 1, -1, -1):
        solved = scaled[height] - ratios[height] * next_one - seconds[height] * next_two
        solution[height] = solved
        next_two, next_one = (next_one, solved)
    return jnp.stack(solution)


def per_device(
    prognostic, metric, first_flux, second_flux, neighbour_face, orientation, coupling, damping
):
    own_traces = face_traces(prognostic)
    extent_first = own_traces.shape[4]
    extent_second = own_traces.shape[5]
    padded = extended(own_traces, (("hx", 5), ("hy", 4)), 1)
    west_outer = pick_face(
        padded[..., 0:extent_first, 1 : extent_second + 1], neighbour_face[0], orientation[0]
    )
    east_outer = pick_face(
        padded[..., 2:, 1 : extent_second + 1], neighbour_face[1], orientation[1]
    )
    south_outer = pick_face(
        padded[..., 1 : extent_first + 1, 0:extent_second], neighbour_face[2], orientation[2]
    )
    north_outer = pick_face(
        padded[..., 1 : extent_first + 1, 2:], neighbour_face[3], orientation[3]
    )
    outer_traces = jnp.stack([west_outer, east_outer, south_outer, north_outer], axis=2)
    section_state = section_values(prognostic, outer_traces, metric, first_flux, second_flux)
    columns = lax.all_to_all(section_state[3:5], "vz", split_axis=2, concat_axis=1, tiled=True)
    source = columns[0] - gravity_couple * level_difference(columns[1])
    centre = coupling[0] + coupling[1] + coupling[2] + coupling[3] + damping[None]
    vertical_speed = solve_unrolled(
        -coupling[0], -coupling[1], centre, -coupling[2], -coupling[3], source
    )
    speed_jump = level_difference(vertical_speed)
    returned = lax.all_to_all(
        jnp.stack([vertical_speed, speed_jump]), "vz", split_axis=1, concat_axis=2, tiled=True
    )
    speed_here = returned[0]
    jump_here = returned[1]
    return jnp.stack(
        [
            section_state[0] - density_couple * jump_here,
            section_state[1],
            section_state[2],
            speed_here,
            section_state[4] - theta_couple * jump_here,
        ]
    )


def solution(mesh):
    placed = (
        P(None, "vz", None, None, "hy", "hx"),
        P(None, None, "hy", "hx"),
        P(),
        P(),
        P(None, "hy", "hx"),
        P(None, "hy", "hx"),
        P(None, None, "vz", None, "hy", "hx"),
        P("vz", None, "hy", "hx"),
    )
    return jax.shard_map(
        per_device,
        mesh=mesh,
        in_specs=placed,
        out_specs=P(None, "vz", None, None, "hy", "hx"),
        check_vma=False,
    )
```

profile of v0, /device:TPU:1, one launch (start us, length us, event | category | flops | bytes accessed | tf_op | source)
XLA Modules:
  0.0 184.2 jit_solution(2517463103171061723)
XLA Ops:
  0.0 1.3 fusion.1374
  1.3 1.3 fusion.1375
  3.1 1.5 fusion.1372
  4.7 2.0 %copy.1166 = f32[5,20,4,4,1,1]{1,3,5,4,2,0:T(4,128)S(1)} copy(f32[5,20,4,4,1,1]{5,0,3,1,4,2:T(8,128)} %get-tuple-element.737) | data formatting | bytes 12800 | tf_op jit(solution)/shard_map/slice | solution.py:20
  6.7 4.4 %collective-permute-start = (f32[5,20,4,4,1,1]{1,3,5,4,2,0:T(4,128)S(1)}, f32[5,20,4,4,1,1]{1,3,5,4,2,0:T(4,128)S(1)}, u32[]{:S(2)}, u32[]{:S(2)}) collective-permute-start(f32[5,20,4,4,1,1]{1,3,5,4,2,0:T(4,128)S(1)} %copy.1166), channel_id=1, source_target_pairs={{0,16},{16,32},{32,48},{48,64},{64,80},{80,96},{96,112},{112,128},... | collective-permute-start | bytes 19208 | tf_op jit(solution)/shard_map/ppermute | solution.py:22
  11.1 1.3 copy.1167
  12.4 13.6 %collective-permute-start.1 = (f32[5,20,4,4,1,1]{1,3,5,4,2,0:T(4,128)}, f32[5,20,4,4,1,1]{1,3,5,4,2,0:T(4,128)}, u32[]{:S(2)}, u32[]{:S(2)}) collective-permute-start(f32[5,20,4,4,1,1]{1,3,5,4,2,0:T(4,128)} %copy.1167), channel_id=1, source_target_pairs={{16,0},{32,16},{48,32},{64,48},{80,64},{96,80},{112,96},{128,112},... | collective-permute-start | bytes 19208 | tf_op jit(solution)/shard_map/ppermute | solution.py:23
  26.0 1.6 fusion.2
  27.7 0.9 fusion.40
  28.6 0.8 slice_bitcast_fusion.2
  30.0 1.6 fusion
  31.8 0.9 slice_negate_fusion.2
  32.7 2.9 %fusion.12 = f32[5,20,4,128,4]{3,4,2,1,0:T(4,128)} fusion(f32[4,4,1,1,1]{1,0,4,3,2:T(4,128)S(1)} %copy-done.59, f32[5,20,4,4,128]{4,0,3,2,1:T(8,128)S(1)} %fusion), kind=kOutput, calls=%fused_computation.22 | convolution fusion | flops 9830400 | bytes 1638464 | tf_op jit(solution)/shard_map/cj,fljiab->flciab/dot_general | solution.py:69
  35.6 0.9 slice_negate_fusion.4
  37.7 2.4 %copy.1168 = f32[5,20,4,4,1,1]{5,0,3,1,4,2:T(8,128)} copy(f32[5,20,4,4,1,1]{1,3,5,4,2,0:T(4,128)S(1)} %collective-permute-done) | data formatting | bytes 12800 | tf_op jit(solution)/shard_map/ppermute | solution.py:22
  40.1 2.2 %copy.1169 = f32[5,20,4,4,1,1]{5,0,3,1,4,2:T(8,128)S(1)} copy(f32[5,20,4,4,1,1]{1,3,5,4,2,0:T(4,128)} %collective-permute-done.1) | data formatting | bytes 12800 | tf_op jit(solution)/shard_map/ppermute | solution.py:23
  42.2 2.4 %pad_maximum_fusion = f32[5,20,4,4,1,130]{5,0,3,1,4,2:T(8,128)S(1)} fusion(f32[5,20,4,4,1,1]{5,0,3,1,4,2:T(8,128)S(1)} %copy.1169, f32[5,20,1,4,1,128]{5,0,3,1,4,2:T(8,128)S(1)} %copy.1567, f32[5,20,1,4,1,128]{5,0,3,1,4,2:T(8,128)S(1)} %copy.1566, f32[5,20,1,4,1,128]{5,0,3,1,4,2:T(8,128)S(1)} %get-tuple-element.861, ...), kind=kLoop, calls=%fused_computation | loop fusion | flops 1040000 | bytes 1664000 | tf_op jit(solution)/shard_map/concatenate | solution.py:24
  45.4 3.2 %collective-permute-start.2 = (f32[5,20,4,4,1,130]{5,3,4,2,1,0:T(4,128)S(1)}, f32[5,20,4,4,1,130]{5,3,4,2,1,0:T(4,128)S(1)}, u32[]{:S(2)}, u32[]{:S(2)}) collective-permute-start(f32[5,20,4,4,1,130]{5,3,4,2,1,0:T(4,128)S(1)} %copy.1170), channel_id=1, source_target_pairs={{0,4},{4,8},{8,12},{12,0},{1,5},{5,9},{9,13},{13,1},{2,6},{6,10},{... | collective-permute-start | bytes 2496008 | tf_op jit(solution)/shard_map/ppermute | solution.py:22
  48.6 3.6 %collective-permute-start.3 = (f32[5,20,4,4,1,130]{5,3,4,2,1,0:T(4,128)S(1)}, f32[5,20,4,4,1,130]{5,3,4,2,1,0:T(4,128)S(1)}, u32[]{:S(2)}, u32[]{:S(2)}) collective-permute-start(f32[5,20,4,4,1,130]{5,3,4,2,1,0:T(4,128)S(1)} %copy.1170), channel_id=1, source_target_pairs={{4,0},{8,4},{12,8},{0,12},{5,1},{9,5},{13,9},{1,13},{6,2},{10,6},{... | collective-permute-start | bytes 2496008 | tf_op jit(solution)/shard_map/ppermute | solution.py:23
  53.0 0.7 fusion.25
  53.8 0.7 convolution_bitcast_fusion.1
  54.6 27.8 %collective-permute-done.2 = f32[5,20,4,4,1,130]{5,3,4,2,1,0:T(4,128)S(1)} collective-permute-done((f32[5,20,4,4,1,130]{5,3,4,2,1,0:T(4,128)S(1)}, f32[5,20,4,4,1,130]{5,3,4,2,1,0:T(4,128)S(1)}, u32[]{:S(2)}, u32[]{:S(2)}) %collective-permute-start.2) | collective-permute-done | bytes 832032 | tf_op jit(solution)/shard_map/ppermute | solution.py:22
  83.3 2.2 %collective-permute-done.3 = f32[5,20,4,4,1,130]{5,3,4,2,1,0:T(4,128)S(1)} collective-permute-done((f32[5,20,4,4,1,130]{5,3,4,2,1,0:T(4,128)S(1)}, f32[5,20,4,4,1,130]{5,3,4,2,1,0:T(4,128)S(1)}, u32[]{:S(2)}, u32[]{:S(2)}) %collective-permute-start.3) | collective-permute-done | bytes 832032 | tf_op jit(solution)/shard_map/ppermute | solution.py:23
  86.4 0.7 convolution_bitcast_fusion.2
  89.1 0.7 copy-done.6
  90.0 2.3 %fusion.10 = f32[5,20,4,4,1,128]{5,3,2,1,0,4:T(4,128)S(1)} fusion(f32[5,20,4,4,1,128]{5,3,2,1,0,4:T(4,128)S(1)} %bitcast.7058, f32[4,4,1,1,1]{1,0,4,3,2:T(4,128)S(1)} %copy-done.59, f32[5,20,4,1,1,128]{5,3,2,1,0,4:T(1,128)S(1)} %copy.1183, f32[5,20,4,1,1,128]{5,3,2,1,0,4:T(1,128)S(1)} %copy.1182, f32[5,20,1,4,1,128]{5,3,2,1,0,4:T(4,128)S(1)} %copy.1185, ...), kind=kOutput, calls=%fused_computation.18 | convolution fusion | flops 12083200 | bytes 4104272 | tf_op jit(solution)/shard_map/ci,fljiab->fljcab/dot_general | solution.py:68
  92.5 0.8 copy.1191
  93.2 15.2 %all-to-all-start = ((f32[2,20,4,4,1,128]{5,3,1,0,4,2:T(4,128)}), f32[2,20,4,4,1,128]{5,3,1,0,4,2:T(4,128)S(1)}, u32[]{:S(2)}, u32[]{:S(2)}) async-start(f32[2,20,4,4,1,128]{5,3,1,0,4,2:T(4,128)} %copy.1191), calls=%async_computation | async-start | bytes 655360 | tf_op jit(solution)/shard_map/all_to_all | solution.py:159
  109.3 0.8 fusion.786
  110.0 0.8 bitcast_subtract_fusion.242
  110.9 0.9 bitcast_subtract_fusion.173
  111.8 11.1 %all-to-all-done = f32[2,20,4,4,1,128]{5,3,1,0,4,2:T(4,128)S(1)} async-done(((f32[2,20,4,4,1,128]{5,3,1,0,4,2:T(4,128)}), f32[2,20,4,4,1,128]{5,3,1,0,4,2:T(4,128)S(1)}, u32[]{:S(2)}, u32[]{:S(2)}) %all-to-all-start) | async-done | bytes 327712 | tf_op jit(solution)/shard_map/all_to_all | solution.py:159
  123.4 0.8 fusion.407
  124.1 0.8 fusion.400
  124.9 0.8 fusion.393
  125.6 0.7 fusion.386
  126.4 0.7 fusion.379
  127.1 0.7 fusion.372
  127.9 0.7 fusion.365
  128.6 0.8 fusion.358
  129.4 0.8 fusion.351
  130.1 0.7 fusion.344
  130.9 0.8 fusion.337
  131.6 0.8 fusion.330
  132.4 0.8 fusion.323
  133.5 0.8 fusion.316
  134.3 0.7 fusion.309
  135.0 0.8 fusion.302
  135.8 0.9 bitcast_subtract_fusion.54
  136.7 1.1 fusion.87
  137.8 1.2 bitcast_multiply_fusion.2
  145.7 1.7 fusion.545
  147.5 0.9 multiply_subtract_fusion.109
  148.4 0.7 multiply_subtract_fusion.107
  149.1 0.7 multiply_subtract_fusion.105
  149.8 0.7 multiply_subtract_fusion.103
  151.2 0.7 multiply_subtract_fusion.99
  151.9 0.7 multiply_subtract_fusion.97
  152.6 0.7 multiply_subtract_fusion.95
  153.3 0.7 multiply_subtract_fusion.93
  154.0 0.7 multiply_subtract_fusion.91
  155.6 1.2 multiply_subtract_fusion.50
  158.1 24.8 %all_to_all.30 = f32[2,80,1,4,1,128]{5,3,4,2,0,1:T(4,128)S(1)} all-to-all(f32[2,80,1,4,1,128]{5,3,4,2,0,1:T(4,128)S(1)} %copy.1550), channel_id=1, replica_groups=mesh['hx'=32,'hy'=4,'vz'=4] {'vz'}, dimensions={1} | all-to-all | bytes 655360 | tf_op jit(solution)/shard_map/all_to_all | solution.py:166
  183.1 1.1 pad_maximum_fusion.2
  (240 shorter events, 18.3 us)
Async XLA Ops:
  0.0 30.0 %copy-start = (f32[5,5]{1,0:T(8,128)S(1)}, f32[5,5]{1,0:T(8,128)}, u32[]{:S(2)}) copy-start(f32[5,5]{1,0:T(8,128)} %param.12) | copy-start | bytes 304
  4.7 21.3 %copy-start.1 = (f32[5,20,4,4,1,128]{5,4,3,2,1,0:T(1,128)S(1)}, f32[5,20,4,4,1,128]{5,4,3,2,1,0:T(1,128)}, u32[]{:S(2)}) copy-start(f32[5,20,4,4,1,128]{5,4,3,2,1,0:T(1,128)} %param.9) | copy-start | bytes 2457604
  4.7 21.3 %copy-start.17 = (f32[5,5]{1,0:T(8,128)S(1)}, f32[5,5]{1,0:T(8,128)}, u32[]{:S(2)}) copy-start(f32[5,5]{1,0:T(8,128)} %param.11) | copy-start | bytes 304
  6.7 31.0 %collective-permute-start = (f32[5,20,4,4,1,1]{1,3,5,4,2,0:T(4,128)S(1)}, f32[5,20,4,4,1,1]{1,3,5,4,2,0:T(4,128)S(1)}, u32[]{:S(2)}, u32[]{:S(2)}) collective-permute-start(f32[5,20,4,4,1,1]{1,3,5,4,2,0:T(4,128)S(1)} %copy.1166), channel_id=1, source_target_pairs={{0,16},{16,32},{32,48},{48,64},{64,80},{80,96},{96,112},{112,128},... | collective-permute-start | bytes 19208 | tf_op jit(solution)/shard_map/ppermute | solution.py:22
  12.4 27.7 %collective-permute-start.1 = (f32[5,20,4,4,1,1]{1,3,5,4,2,0:T(4,128)}, f32[5,20,4,4,1,1]{1,3,5,4,2,0:T(4,128)}, u32[]{:S(2)}, u32[]{:S(2)}) collective-permute-start(f32[5,20,4,4,1,1]{1,3,5,4,2,0:T(4,128)} %copy.1167), channel_id=1, source_target_pairs={{16,0},{32,16},{48,32},{64,48},{80,64},{96,80},{112,96},{128,112},... | collective-permute-start | bytes 19208 | tf_op jit(solution)/shard_map/ppermute | solution.py:23
  44.7 7.5 %copy-start.2 = (f32[5,20,4,4,1,1]{5,0,3,1,4,2:T(8,128)S(1)}, f32[5,20,4,4,1,1]{5,0,3,1,4,2:T(8,128)}, u32[]{:S(2)}) copy-start(f32[5,20,4,4,1,1]{5,0,3,1,4,2:T(8,128)} %copy.1168) | copy-start | bytes 19204
  44.7 7.5 %copy-start.67 = (pred[128]{0:T(512)(128)(4,1)S(1)}, pred[128]{0:T(512)(128)(4,1)}, u32[]{:S(2)}) copy-start(pred[128]{0:T(512)(128)(4,1)} %get-tuple-element.851) | copy-start | bytes 388
  44.7 7.5 %copy-start.68 = (pred[128]{0:T(512)(128)(4,1)S(1)}, pred[128]{0:T(512)(128)(4,1)}, u32[]{:S(2)}) copy-start(pred[128]{0:T(512)(128)(4,1)} %get-tuple-element.852) | copy-start | bytes 388
  44.7 7.5 %copy-start.69 = (pred[128]{0:T(512)(128)(4,1)S(1)}, pred[128]{0:T(512)(128)(4,1)}, u32[]{:S(2)}) copy-start(pred[128]{0:T(512)(128)(4,1)} %get-tuple-element.853) | copy-start | bytes 388
  44.7 7.5 %copy-start.70 = (pred[128]{0:T(512)(128)(4,1)S(1)}, pred[128]{0:T(512)(128)(4,1)}, u32[]{:S(2)}) copy-start(pred[128]{0:T(512)(128)(4,1)} %get-tuple-element.859) | copy-start | bytes 388
  45.4 37.0 %collective-permute-start.2 = (f32[5,20,4,4,1,130]{5,3,4,2,1,0:T(4,128)S(1)}, f32[5,20,4,4,1,130]{5,3,4,2,1,0:T(4,128)S(1)}, u32[]{:S(2)}, u32[]{:S(2)}) collective-permute-start(f32[5,20,4,4,1,130]{5,3,4,2,1,0:T(4,128)S(1)} %copy.1170), channel_id=1, source_target_pairs={{0,4},{4,8},{8,12},{12,0},{1,5},{5,9},{9,13},{13,1},{2,6},{6,10},{... | collective-permute-start | bytes 2496008 | tf_op jit(solution)/shard_map/ppermute | solution.py:22
  48.6 36.9 %collective-permute-start.3 = (f32[5,20,4,4,1,130]{5,3,4,2,1,0:T(4,128)S(1)}, f32[5,20,4,4,1,130]{5,3,4,2,1,0:T(4,128)S(1)}, u32[]{:S(2)}, u32[]{:S(2)}) collective-permute-start(f32[5,20,4,4,1,130]{5,3,4,2,1,0:T(4,128)S(1)} %copy.1170), channel_id=1, source_target_pairs={{4,0},{8,4},{12,8},{0,12},{5,1},{9,5},{13,9},{1,13},{6,2},{10,6},{... | collective-permute-start | bytes 2496008 | tf_op jit(solution)/shard_map/ppermute | solution.py:23
  54.5 28.4 %copy-start.60 = (pred[128]{0:T(512)(128)(4,1)S(1)}, pred[128]{0:T(512)(128)(4,1)}, u32[]{:S(2)}) copy-start(pred[128]{0:T(512)(128)(4,1)} %get-tuple-element.845) | copy-start | bytes 388
  54.5 28.4 %copy-start.61 = (pred[128]{0:T(512)(128)(4,1)S(1)}, pred[128]{0:T(512)(128)(4,1)}, u32[]{:S(2)}) copy-start(pred[128]{0:T(512)(128)(4,1)} %get-tuple-element.846) | copy-start | bytes 388
  54.5 28.4 %copy-start.62 = (pred[128]{0:T(512)(128)(4,1)S(1)}, pred[128]{0:T(512)(128)(4,1)}, u32[]{:S(2)}) copy-start(pred[128]{0:T(512)(128)(4,1)} %get-tuple-element.847) | copy-start | bytes 388
  54.6 28.7 %copy-start.74 = (pred[128]{0:T(512)(128)(4,1)S(1)}, pred[128]{0:T(512)(128)(4,1)}, u32[]{:S(2)}) copy-start(pred[128]{0:T(512)(128)(4,1)} %get-tuple-element.840) | copy-start | bytes 388
  92.3 16.2 %copy-start.8 = (f32[4,80,1,4,1,128]{5,4,3,2,1,0:T(1,128)S(1)}, f32[4,80,1,4,1,128]{5,4,3,2,1,0:T(1,128)}, u32[]{:S(2)}) copy-start(f32[4,80,1,4,1,128]{5,4,3,2,1,0:T(1,128)} %param.15) | copy-start | bytes 1966084
  92.3 16.1 %copy-start.58 = (f32[1,4,1,128]{3,2,1,0:T(1,128)S(1)}, f32[1,4,1,128]{3,2,1,0:T(1,128)}, u32[]{:S(2)}) copy-start(f32[1,4,1,128]{3,2,1,0:T(1,128)} %param.16) | copy-start | bytes 6148
  92.4 16.2 %copy-start.3 = (f32[1,80,1,4,1,128]{5,3,4,2,1,0:T(4,128)S(1)}, f32[1,80,1,4,1,128]{5,3,4,2,1,0:T(4,128)}, u32[]{:S(2)}) copy-start(f32[1,80,1,4,1,128]{5,3,4,2,1,0:T(4,128)} %get-tuple-element.750) | copy-start | bytes 491524
  92.4 16.2 %copy-start.4 = (f32[1,80,1,4,1,128]{5,3,4,2,1,0:T(4,128)S(1)}, f32[1,80,1,4,1,128]{5,3,4,2,1,0:T(4,128)}, u32[]{:S(2)}) copy-start(f32[1,80,1,4,1,128]{5,3,4,2,1,0:T(4,128)} %get-tuple-element.748) | copy-start | bytes 491524
  92.4 16.2 %copy-start.9 = (f32[1,80,1,4,1,128]{5,3,4,2,1,0:T(4,128)S(1)}, f32[1,80,1,4,1,128]{5,3,4,2,1,0:T(4,128)}, u32[]{:S(2)}) copy-start(f32[1,80,1,4,1,128]{5,3,4,2,1,0:T(4,128)} %get-tuple-element.749) | copy-start | bytes 491524
  92.4 16.2 %copy-start.10 = (f32[1,80,1,4,1,128]{5,3,4,2,1,0:T(4,128)S(1)}, f32[1,80,1,4,1,128]{5,3,4,2,1,0:T(4,128)}, u32[]{:S(2)}) copy-start(f32[1,80,1,4,1,128]{5,3,4,2,1,0:T(4,128)} %get-tuple-element.747) | copy-start | bytes 491524
  93.2 29.7 %all-to-all-start = ((f32[2,20,4,4,1,128]{5,3,1,0,4,2:T(4,128)}), f32[2,20,4,4,1,128]{5,3,1,0,4,2:T(4,128)S(1)}, u32[]{:S(2)}, u32[]{:S(2)}) async-start(f32[2,20,4,4,1,128]{5,3,1,0,4,2:T(4,128)} %copy.1191), calls=%async_computation | async-start | bytes 655360 | tf_op jit(solution)/shard_map/all_to_all | solution.py:159
  108.6 14.8 %copy-start.11 = (f32[80,1,4,1,128]{4,2,3,1,0:T(4,128)}, f32[80,1,4,1,128]{4,2,3,1,0:T(4,128)S(1)}, u32[]{:S(2)}) copy-start(f32[80,1,4,1,128]{4,2,3,1,0:T(4,128)S(1)} %bitcast_add_fusion) | copy-start | bytes 491524
  133.1 12.2 %copy-start.18 = (f32[4,128]{1,0:T(4,128)S(1)}, f32[4,128]{1,0:T(4,128)}, u32[]{:S(2)}) copy-start(f32[4,128]{1,0:T(4,128)} %get-tuple-element.692) | copy-start | bytes 6148
  133.1 12.2 %copy-start.19 = (f32[4,128]{1,0:T(4,128)S(1)}, f32[4,128]{1,0:T(4,128)}, u32[]{:S(2)}) copy-start(f32[4,128]{1,0:T(4,128)} %get-tuple-element.693) | copy-start | bytes 6148
  133.2 12.2 %copy-start.20 = (f32[4,128]{1,0:T(4,128)S(1)}, f32[4,128]{1,0:T(4,128)}, u32[]{:S(2)}) copy-start(f32[4,128]{1,0:T(4,128)} %get-tuple-element.698) | copy-start | bytes 6148
  133.2 12.2 %copy-start.21 = (f32[4,128]{1,0:T(4,128)S(1)}, f32[4,128]{1,0:T(4,128)}, u32[]{:S(2)}) copy-start(f32[4,128]{1,0:T(4,128)} %get-tuple-element.699) | copy-start | bytes 6148
  133.2 12.2 %copy-start.22 = (f32[4,128]{1,0:T(4,128)S(1)}, f32[4,128]{1,0:T(4,128)}, u32[]{:S(2)}) copy-start(f32[4,128]{1,0:T(4,128)} %get-tuple-element.704) | copy-start | bytes 6148
  133.2 12.2 %copy-start.23 = (f32[4,128]{1,0:T(4,128)S(1)}, f32[4,128]{1,0:T(4,128)}, u32[]{:S(2)}) copy-start(f32[4,128]{1,0:T(4,128)} %get-tuple-element.705) | copy-start | bytes 6148
  133.2 12.2 %copy-start.24 = (f32[4,128]{1,0:T(4,128)S(1)}, f32[4,128]{1,0:T(4,128)}, u32[]{:S(2)}) copy-start(f32[4,128]{1,0:T(4,128)} %get-tuple-element.573) | copy-start | bytes 6148
  133.2 12.2 %copy-start.25 = (f32[4,128]{1,0:T(4,128)S(1)}, f32[4,128]{1,0:T(4,128)}, u32[]{:S(2)}) copy-start(f32[4,128]{1,0:T(4,128)} %get-tuple-element.574) | copy-start | bytes 6148
  133.2 12.2 %copy-start.26 = (f32[4,128]{1,0:T(4,128)S(1)}, f32[4,128]{1,0:T(4,128)}, u32[]{:S(2)}) copy-start(f32[4,128]{1,0:T(4,128)} %get-tuple-element.579) | copy-start | bytes 6148
  133.2 12.2 %copy-start.27 = (f32[4,128]{1,0:T(4,128)S(1)}, f32[4,128]{1,0:T(4,128)}, u32[]{:S(2)}) copy-start(f32[4,128]{1,0:T(4,128)} %get-tuple-element.580) | copy-start | bytes 6148
  133.2 12.2 %copy-start.28 = (f32[4,128]{1,0:T(4,128)S(1)}, f32[4,128]{1,0:T(4,128)}, u32[]{:S(2)}) copy-start(f32[4,128]{1,0:T(4,128)} %get-tuple-element.585) | copy-start | bytes 6148
  133.2 12.2 %copy-start.29 = (f32[4,128]{1,0:T(4,128)S(1)}, f32[4,128]{1,0:T(4,128)}, u32[]{:S(2)}) copy-start(f32[4,128]{1,0:T(4,128)} %get-tuple-element.586) | copy-start | bytes 6148
  133.3 12.2 %copy-start.30 = (f32[4,128]{1,0:T(4,128)S(1)}, f32[4,128]{1,0:T(4,128)}, u32[]{:S(2)}) copy-start(f32[4,128]{1,0:T(4,128)} %get-tuple-element.591) | copy-start | bytes 6148
  133.3 12.2 %copy-start.31 = (f32[4,128]{1,0:T(4,128)S(1)}, f32[4,128]{1,0:T(4,128)}, u32[]{:S(2)}) copy-start(f32[4,128]{1,0:T(4,128)} %get-tuple-element.592) | copy-start | bytes 6148
  133.3 12.2 %copy-start.32 = (f32[4,128]{1,0:T(4,128)S(1)}, f32[4,128]{1,0:T(4,128)}, u32[]{:S(2)}) copy-start(f32[4,128]{1,0:T(4,128)} %get-tuple-element.597) | copy-start | bytes 6148
  133.3 12.2 %copy-start.33 = (f32[4,128]{1,0:T(4,128)S(1)}, f32[4,128]{1,0:T(4,128)}, u32[]{:S(2)}) copy-start(f32[4,128]{1,0:T(4,128)} %get-tuple-element.598) | copy-start | bytes 6148
  133.3 12.2 %copy-start.34 = (f32[4,128]{1,0:T(4,128)S(1)}, f32[4,128]{1,0:T(4,128)}, u32[]{:S(2)}) copy-start(f32[4,128]{1,0:T(4,128)} %get-tuple-element.603) | copy-start | bytes 6148
  133.3 12.2 %copy-start.35 = (f32[4,128]{1,0:T(4,128)S(1)}, f32[4,128]{1,0:T(4,128)}, u32[]{:S(2)}) copy-start(f32[4,128]{1,0:T(4,128)} %get-tuple-element.604) | copy-start | bytes 6148
  133.3 12.2 %copy-start.36 = (f32[4,128]{1,0:T(4,128)S(1)}, f32[4,128]{1,0:T(4,128)}, u32[]{:S(2)}) copy-start(f32[4,128]{1,0:T(4,128)} %get-tuple-element.609) | copy-start | bytes 6148
  133.3 12.2 %copy-start.37 = (f32[4,128]{1,0:T(4,128)S(1)}, f32[4,128]{1,0:T(4,128)}, u32[]{:S(2)}) copy-start(f32[4,128]{1,0:T(4,128)} %get-tuple-element.610) | copy-start | bytes 6148
  133.3 12.2 %copy-start.38 = (f32[4,128]{1,0:T(4,128)S(1)}, f32[4,128]{1,0:T(4,128)}, u32[]{:S(2)}) copy-start(f32[4,128]{1,0:T(4,128)} %get-tuple-element.615) | copy-start | bytes 6148
  133.3 12.2 %copy-start.39 = (f32[4,128]{1,0:T(4,128)S(1)}, f32[4,128]{1,0:T(4,128)}, u32[]{:S(2)}) copy-start(f32[4,128]{1,0:T(4,128)} %get-tuple-element.616) | copy-start | bytes 6148
  133.4 12.2 %copy-start.40 = (f32[4,128]{1,0:T(4,128)S(1)}, f32[4,128]{1,0:T(4,128)}, u32[]{:S(2)}) copy-start(f32[4,128]{1,0:T(4,128)} %get-tuple-element.621) | copy-start | bytes 6148
  133.4 12.2 %copy-start.41 = (f32[4,128]{1,0:T(4,128)S(1)}, f32[4,128]{1,0:T(4,128)}, u32[]{:S(2)}) copy-start(f32[4,128]{1,0:T(4,128)} %get-tuple-element.622) | copy-start | bytes 6148
  133.4 12.2 %copy-start.42 = (f32[4,128]{1,0:T(4,128)S(1)}, f32[4,128]{1,0:T(4,128)}, u32[]{:S(2)}) copy-start(f32[4,128]{1,0:T(4,128)} %get-tuple-element.627) | copy-start | bytes 6148
  133.4 12.2 %copy-start.43 = (f32[4,128]{1,0:T(4,128)S(1)}, f32[4,128]{1,0:T(4,128)}, u32[]{:S(2)}) copy-start(f32[4,128]{1,0:T(4,128)} %get-tuple-element.628) | copy-start | bytes 6148
  133.4 12.2 %copy-start.44 = (f32[4,128]{1,0:T(4,128)S(1)}, f32[4,128]{1,0:T(4,128)}, u32[]{:S(2)}) copy-start(f32[4,128]{1,0:T(4,128)} %get-tuple-element.633) | copy-start | bytes 6148
  133.4 12.2 %copy-start.45 = (f32[4,128]{1,0:T(4,128)S(1)}, f32[4,128]{1,0:T(4,128)}, u32[]{:S(2)}) copy-start(f32[4,128]{1,0:T(4,128)} %get-tuple-element.634) | copy-start | bytes 6148
  133.4 12.2 %copy-start.46 = (f32[4,128]{1,0:T(4,128)S(1)}, f32[4,128]{1,0:T(4,128)}, u32[]{:S(2)}) copy-start(f32[4,128]{1,0:T(4,128)} %get-tuple-element.860) | copy-start | bytes 6148
  133.4 12.2 %copy-start.47 = (f32[4,128]{1,0:T(4,128)S(1)}, f32[4,128]{1,0:T(4,128)}, u32[]{:S(2)}) copy-start(f32[4,128]{1,0:T(4,128)} %get-tuple-element.499) | copy-start | bytes 6148
  133.4 12.2 %copy-start.48 = (f32[4,128]{1,0:T(4,128)S(1)}, f32[4,128]{1,0:T(4,128)}, u32[]{:S(2)}) copy-start(f32[4,128]{1,0:T(4,128)} %get-tuple-element.502) | copy-start | bytes 6148
  133.4 12.2 %copy-start.49 = (f32[4,128]{1,0:T(4,128)S(1)}, f32[4,128]{1,0:T(4,128)}, u32[]{:S(2)}) copy-start(f32[4,128]{1,0:T(4,128)} %get-tuple-element.507) | copy-start | bytes 6148
  133.5 12.2 %copy-start.50 = (f32[4,128]{1,0:T(4,128)S(1)}, f32[4,128]{1,0:T(4,128)}, u32[]{:S(2)}) copy-start(f32[4,128]{1,0:T(4,128)} %get-tuple-element.508) | copy-start | bytes 6148
  133.5 12.2 %copy-start.51 = (f32[4,128]{1,0:T(4,128)S(1)}, f32[4,128]{1,0:T(4,128)}, u32[]{:S(2)}) copy-start(f32[4,128]{1,0:T(4,128)} %get-tuple-element.513) | copy-start | bytes 6148
  133.5 12.2 %copy-start.52 = (f32[4,128]{1,0:T(4,128)S(1)}, f32[4,128]{1,0:T(4,128)}, u32[]{:S(2)}) copy-start(f32[4,128]{1,0:T(4,128)} %get-tuple-element.514) | copy-start | bytes 6148
  133.5 12.2 %copy-start.53 = (f32[4,128]{1,0:T(4,128)S(1)}, f32[4,128]{1,0:T(4,128)}, u32[]{:S(2)}) copy-start(f32[4,128]{1,0:T(4,128)} %get-tuple-element.519) | copy-start | bytes 6148
  133.5 12.2 %copy-start.54 = (f32[4,128]{1,0:T(4,128)S(1)}, f32[4,128]{1,0:T(4,128)}, u32[]{:S(2)}) copy-start(f32[4,128]{1,0:T(4,128)} %get-tuple-element.520) | copy-start | bytes 6148
  133.5 12.2 %copy-start.55 = (f32[4,128]{1,0:T(4,128)S(1)}, f32[4,128]{1,0:T(4,128)}, u32[]{:S(2)}) copy-start(f32[4,128]{1,0:T(4,128)} %get-tuple-element.525) | copy-start | bytes 6148
  133.5 12.2 %copy-start.56 = (f32[4,128]{1,0:T(4,128)S(1)}, f32[4,128]{1,0:T(4,128)}, u32[]{:S(2)}) copy-start(f32[4,128]{1,0:T(4,128)} %get-tuple-element.526) | copy-start | bytes 6148
  133.5 12.2 %copy-start.57 = (f32[4,128]{1,0:T(4,128)S(1)}, f32[4,128]{1,0:T(4,128)}, u32[]{:S(2)}) copy-start(f32[4,128]{1,0:T(4,128)} %get-tuple-element.531) | copy-start | bytes 6148
  (20 other events, 29.5 us)
where the time goes:
time: 186 us; the launch traced here: 184 us
  other arithmetic  46.4 us (25%)
  waiting for transfers between devices  41.2 us (22%)
  starting transfers between devices  40 us (22%)
  blocking collectives  24.8 us (13%)
  local copies, waits for them, and re-layouts  20.3 us (11%)
  matrix products  9.88 us (5%)
    ppermute x2, waiting for transfers between devices, extended(): before = lax.ppermute(last, axis, up)  27.8 us
    all_to_all x1, blocking collectives, per_device(): lax.all_to_all(jnp.stack([vertical_speed, speed_jump]), 'vz', split_axis=...  24.8 us
    ppermute x2, starting transfers between devices, extended(): after = lax.ppermute(initial, axis, down)  17.2 us
    all_to_all x1, starting transfers between devices, per_device(): lax.all_to_all(section_state[3:5], 'vz', split_axis=2, concat_axis=1, til...  15.2 us
    sub x34, other arithmetic, solve_unrolled(): scaled[height] - ratios[height] * next_one - seconds[height] * next_two  14.2 us
    div x21, other arithmetic, solve_unrolled(): (source[height] - entry_a[height] * far_value - reduced * near_value) / p...  13.8 us
    all_to_all x1, waiting for transfers between devices, per_device(): lax.all_to_all(section_state[3:5], 'vz', split_axis=2, concat_axis=1, til...  11.1 us
    ppermute x2, starting transfers between devices, extended(): before = lax.ppermute(last, axis, up)  7.56 us
  transfers between devices with their start and end apart: 5, of which 3 were waited for; matrix products, arithmetic and copies ran while one was open for 12% of the time, Pallas kernels for 0%

commit v1 on v0

v1 whole, which is shorter than its diff:
```python
import functools

import jax
import jax.numpy as jnp
import numpy as np
from jax import lax
from jax.experimental import pallas as pl
from jax.experimental.pallas import tpu as pltpu
from jax.sharding import PartitionSpec as P

step_size = 0.05
lift_weight = 6.0
gravity_couple = 0.5
density_couple = 0.3
theta_couple = 0.4

FIELDS = 5
ROWS = 8
LANES = 128


def derivative_matrix():
    points = np.array([-1.0, -1.0 / np.sqrt(5.0), 1.0 / np.sqrt(5.0), 1.0])
    number = points.shape[0]
    barycentric = np.ones(number)
    for source in range(number):
        for another in range(number):
            if another != source:
                barycentric[source] = barycentric[source] / (points[source] - points[another])
    matrix = np.zeros((number, number))
    for target in range(number):
        for source in range(number):
            if target != source:
                matrix[target, source] = (
                    barycentric[source] / barycentric[target] / (points[target] - points[source])
                )
        matrix[target, target] = -np.sum(matrix[target])
    return matrix


def weight_table():
    d = derivative_matrix()
    half = 0.5 * lift_weight
    along = np.zeros((7, ROWS))
    for row in range(ROWS):
        i = row % 4
        for offset in range(-3, 4):
            if 0 <= i + offset < 4:
                along[offset + 3, row] = -d[i, i + offset]
    cx = np.array([{0: -half, 3: half}.get(r % 4, 0.0) for r in range(ROWS)])
    along[3] += cx
    across = np.zeros((2, 2, 2, ROWS))
    for tile in range(2):
        for other in range(2):
            for row in range(ROWS):
                jl = row // 4
                j = 2 * tile + jl
                across[tile, other, 0, row] = -d[j, 2 * other + jl]
                across[tile, other, 1, row] = -d[j, 2 * other + 1 - jl]
    cy = np.zeros((2, ROWS))
    cy[0, :4] = -half
    cy[1, 4:] = half
    for tile in range(2):
        across[tile, tile, 0] += cy[tile]
    own = np.zeros((2, ROWS))
    for tile in range(2):
        own[tile] = -np.abs(cx) - np.abs(cy[tile])
    rows = np.concatenate(
        [along, across.reshape(8, ROWS), cx[None], np.abs(cx)[None], cy, np.abs(cy), own]
    )
    return np.ascontiguousarray(
        np.broadcast_to(rows[:, :, None], rows.shape + (LANES,)).astype(np.float32)
    )


def rows_of(shape=(ROWS, LANES)):
    return lax.broadcasted_iota(jnp.int32, shape, 0)


def lanes_of(shape=(ROWS, LANES)):
    return lax.broadcasted_iota(jnp.int32, shape, 1)


def spread(row):
    return jnp.broadcast_to(row, (ROWS, LANES))


def node_rows(face, flip):
    k = rows_of() % 4
    k = jnp.where(flip == 1, 3 - k, k)
    return jnp.where(
        face == 0, 4 * k, jnp.where(face == 1, 4 * k + 3, jnp.where(face == 2, k, 12 + k))
    )


def take_rows(tile, index):
    return jnp.take_along_axis(tile, index, axis=0, mode="promise_in_bounds")


def take_nodes(low, high, node):
    index = jnp.where(node >= ROWS, node - ROWS, node)
    return jnp.where(node >= ROWS, take_rows(high, index), take_rows(low, index))


def halves(low, high):
    return jnp.where(rows_of() < 4, low, high)


def pack_faces(state, tables, north_message, south_message):
    levels = state.shape[1]
    node = halves(
        node_rows(spread(tables[0:1]), spread(tables[1:2])),
        node_rows(spread(tables[2:3]), spread(tables[3:4])),
    )

    def at(count, carry):
        for field in range(FIELDS):
            chosen = take_nodes(
                state[field, count, 0:ROWS], state[field, count, ROWS : 2 * ROWS], node
            )
            north_message[field, count] = chosen[0:4]
            south_message[field, count] = chosen[4:8]
        return carry

    lax.fori_loop(0, levels, at, 0, unroll=2)


def pack_edges(state, edges):
    levels = state.shape[1]
    lane = lanes_of()
    zero = state[0, 0, 0:ROWS] - state[0, 0, 0:ROWS]

    def at(count, held):
        held = list(held)
        for field in range(FIELDS):
            number = field * levels + count
            at_first = lane == number
            at_last = lane == lax.rem(number + LANES - 1, LANES)
            for tile in range(2):
                moved = pltpu.roll(
                    state[field, count, tile * ROWS : (tile + 1) * ROWS], number, 1
                )
                held[tile] = jnp.where(at_first, moved, held[tile])
                held[2 + tile] = jnp.where(at_last, moved, held[2 + tile])
        return tuple(held)

    held = lax.fori_loop(0, levels, at, (zero,) * 4)
    for tile in range(2):
        edges[0, tile * ROWS : (tile + 1) * ROWS] = held[tile]
        edges[1, tile * ROWS : (tile + 1) * ROWS] = held[2 + tile]


def edge_values(before, after, faces, flips):
    def lane_value(table, row, lane):
        return jnp.broadcast_to(table[row : row + 1, lane : lane + 1], (ROWS, LANES))

    from_before = take_nodes(
        before[0:ROWS],
        before[ROWS : 2 * ROWS],
        node_rows(lane_value(faces, 2, 0), lane_value(flips, 2, 0)),
    )
    from_after = take_nodes(
        after[0:ROWS],
        after[ROWS : 2 * ROWS],
        node_rows(lane_value(faces, 3, LANES - 1), lane_value(flips, 3, LANES - 1)),
    )
    return halves(pltpu.roll(from_before, 1, 1), pltpu.roll(from_after, LANES - 1, 1))


def make_section(
    state, scale, first, second, faces, flips, west, east, before, after, weights, section
):
    levels = state.shape[1]
    row, lane = rows_of(), lanes_of()
    node = halves(
        node_rows(
            pltpu.roll(spread(faces[2:3]), LANES - 1, 1),
            pltpu.roll(spread(flips[2:3]), LANES - 1, 1),
        ),
        node_rows(pltpu.roll(spread(faces[3:4]), 1, 1), pltpu.roll(spread(flips[3:4]), 1, 1)),
    )
    edge = edge_values(before, after, faces, flips)
    at_edge = ((row < 4) & (lane == 0)) | ((row >= 4) & (lane == LANES - 1))
    left = row % 4 < 2
    place = [jnp.where(left, 2 * tile + row // 4, 4 + 2 * tile + row // 4) for tile in range(2)]

    def at(count, carry):
        q1 = [[None] * 2 for _ in range(FIELDS)]
        q2 = [[None] * 2 for _ in range(FIELDS)]
        rest = [[None] * 2 for _ in range(FIELDS)]
        own = [[None] * 2 for _ in range(FIELDS)]
        for field in range(FIELDS):
            number = field * levels + count
            tiles = [state[field, count, t * ROWS : (t + 1) * ROWS] for t in range(2)]
            swapped = [pltpu.roll(tile, 4, 0) for tile in tiles]
            chosen = take_nodes(tiles[0], tiles[1], node)
            across = halves(pltpu.roll(chosen, 1, 1), pltpu.roll(chosen, LANES - 1, 1))
            shift = lax.rem(2 * LANES - number, LANES)
            across = jnp.where(at_edge, pltpu.roll(edge, shift, 1), across)
            sides = jnp.concatenate([west[field, count], east[field, count]], axis=0)
            for t in range(2):
                along = take_rows(sides, place[t])
                total = weights[3] * tiles[t] - weights[15] * along
                for offset in (-3, -2, -1, 1, 2, 3):
                    total += weights[offset + 3] * pltpu.roll(tiles[t], (-offset) % ROWS, 0)
                q1[field][t] = total
                total = -weights[17 + t] * across
                for other in range(2):
                    total += weights[7 + 4 * t + 2 * other] * tiles[other]
                    total += weights[8 + 4 * t + 2 * other] * swapped[other]
                q2[field][t] = total
                rest[field][t] = (
                    weights[21 + t] * tiles[t] + weights[16] * along + weights[19 + t] * across
                )
                own[field][t] = tiles[t]
        for field in range(FIELDS):
            for t in range(2):
                total = rest[field][t]
                for other in range(FIELDS):
                    total += first[field, other] * q1[other][t]
                    total += second[field, other] * q2[other][t]
                section[field, count, t * ROWS : (t + 1) * ROWS] = (
                    own[field][t] + step_size * scale[t * ROWS : (t + 1) * ROWS] * total
                )
        return carry

    lax.fori_loop(0, levels, at, 0)


def column_message(section, message):
    levels = section.shape[1]
    for t in range(2):
        span = slice(t * ROWS, (t + 1) * ROWS)
        warm = [section[4, count, span] for count in range(levels)]
        entries = []
        for count in range(levels):
            total = section[3, count, span]
            if count + 1 < levels:
                total = total - gravity_couple * warm[count + 1]
            if count > 0:
                total = total + gravity_couple * warm[count - 1]
            entries.append(total)
        entries += [warm[0], warm[levels - 1]]
        for count, entry in enumerate(entries):
            message[2 * t, count] = entry[0:4]
            message[2 * t + 1, count] = entry[4:8]


def pair(low, high):
    return jnp.concatenate([low, high], axis=0)


def factor(coupling, damping, factors):
    levels = coupling.shape[1]
    half = levels // 2
    damp = pair(damping[...], damping[...])
    zero = damp - damp

    def at(t, carry):
        far_ratio, far_second, near_ratio, near_second = carry
        up = levels - 1 - t
        entry_a = pair(coupling[0, t], coupling[3, up])
        entry_b = pair(coupling[1, t], coupling[2, up])
        entry_d = pair(coupling[2, t], coupling[1, up])
        entry_e = pair(coupling[3, t], coupling[0, up])
        centre = entry_a + entry_b + entry_d + entry_e + damp
        reduced = entry_a * far_ratio - entry_b
        pivot = centre + entry_a * far_second - reduced * near_ratio
        inverse = 1.0 / pivot
        ratio = -(entry_d + reduced * near_second) * inverse
        second = -entry_e * inverse
        factors[0, t] = inverse
        factors[1, t] = entry_a * inverse
        factors[2, t] = reduced * inverse
        factors[3, t] = ratio
        factors[4, t] = second
        return near_ratio, near_second, ratio, second

    lax.fori_loop(0, half, at, (zero,) * 4)


def solve(factors, columns, message):
    parts, count = columns.shape[0], columns.shape[1] - 2
    levels = parts * count
    half = levels // 2

    def source(level):
        d, place = level // count, level % count
        entry = columns[d, place]
        if place == 0 and d > 0:
            entry = entry + gravity_couple * columns[d - 1, count + 1]
        if place == count - 1 and d < parts - 1:
            entry = entry - gravity_couple * columns[d + 1, count]
        return entry

    far = near = jnp.zeros((ROWS, LANES), jnp.float32)
    scaled = []
    for t in range(half):
        entry = pair(source(t), source(levels - 1 - t)) * factors[0, t]
        far, near = near, (entry + factors[1, t] * far) - factors[2, t] * near
        scaled.append(near)
    top, under = half - 1, half - 2
    value_1, value_2 = scaled[top], scaled[under]
    ratio_1, ratio_2 = factors[3, top], factors[3, under]
    second_1, second_2 = factors[4, top], factors[4, under]
    other_value = pltpu.roll(value_2, 4, 0)
    other_ratio = pltpu.roll(ratio_2, 4, 0)
    other_second = pltpu.roll(second_2, 4, 0)
    here = 1.0 - second_1 * other_second
    there = ratio_1 - second_1 * other_ratio
    right = value_1 - second_1 * other_value
    here_2 = pltpu.roll(here, 4, 0)
    there_2 = pltpu.roll(there, 4, 0)
    right_2 = pltpu.roll(right, 4, 0)
    mine = (right * here_2 - there * right_2) / (here * here_2 - there * there_2)
    next_one, next_two = mine, pltpu.roll(mine, 4, 0)
    blank = jnp.zeros((4, LANES), jnp.float32)

    def put(level, entry):
        for d in range(parts):
            place = level - d * count + 1
            if 0 <= place < count + 2:
                message[d, place] = entry

    put(-1, blank)
    put(levels, blank)
    put(top, mine[0:4])
    put(levels - 1 - top, mine[4:8])
    for t in range(half - 2, -1, -1):
        found = (scaled[t] - factors[4, t] * next_two) - factors[3, t] * next_one
        put(t, found[0:4])
        put(levels - 1 - t, found[4:8])
        next_one, next_two = found, next_one


def finish(section, returned, updated):
    levels = section.shape[1]

    def at(count, carry):
        for t in range(2):
            span = slice(t * ROWS, (t + 1) * ROWS)

            def level(place):
                return pair(returned[2 * t, place], returned[2 * t + 1, place])

            jump = level(count + 2) - level(count)
            updated[0, count, span] = section[0, count, span] - density_couple * jump
            updated[1, count, span] = section[1, count, span]
            updated[2, count, span] = section[2, count, span]
            updated[3, count, span] = level(count + 1)
            updated[4, count, span] = section[4, count, span] - theta_couple * jump
        return carry

    lax.fori_loop(0, levels, at, 0, unroll=2)


VM = pl.BlockSpec(memory_space=pltpu.VMEM)
SM = pl.BlockSpec(memory_space=pltpu.SMEM)


def f32(*shape):
    return jax.ShapeDtypeStruct(shape, jnp.float32)


def pack_kernel(state, tables, north_message, south_message, edges):
    pack_faces(state, tables[...], north_message, south_message)
    pack_edges(state, edges)


def section_kernel(
    first, second, state, scale, faces, flips, west, east, before, after, weights, section, message
):
    make_section(
        state,
        scale,
        first,
        second,
        faces[...],
        flips[...],
        west,
        east,
        before[...],
        after[...],
        weights,
        section,
    )
    column_message(section, message)


def per_device(
    prognostic, metric, first_flux, second_flux, neighbour_face, orientation, coupling, damping
):
    levels = prognostic.shape[1]
    parts = lax.axis_size("vz")
    state = prognostic.reshape(FIELDS, levels, 16, LANES)
    scale = metric.reshape(16, LANES)
    faces = neighbour_face.reshape(4, LANES)
    flips = orientation.reshape(4, LANES)
    couples = coupling.reshape(4, levels * parts, 4, LANES)
    damp = damping.reshape(4, LANES)

    def shifted(x, axis, by):
        size = lax.axis_size(axis)
        return lax.ppermute(x, axis, [(i, (i + by) % size) for i in range(size)])

    west_table = shifted(jnp.stack([faces[0], flips[0]]), "hy", -1)
    east_table = shifted(jnp.stack([faces[1], flips[1]]), "hy", 1)
    tables = jnp.concatenate([west_table, east_table])
    factors = pl.pallas_call(
        factor,
        out_shape=f32(5, levels * parts // 2, ROWS, LANES),
        in_specs=[VM, VM],
        out_specs=VM,
        name="factor",
        cost_estimate=pl.CostEstimate(flops=4000000, bytes_accessed=1500000, transcendentals=0),
    )(couples, damp)
    north_message, south_message, edges = pl.pallas_call(
        pack_kernel,
        out_shape=(f32(FIELDS, levels, 4, LANES), f32(FIELDS, levels, 4, LANES), f32(2, 16, LANES)),
        in_specs=[VM, VM],
        out_specs=(VM, VM, VM),
        name="pack",
    )(state, tables)
    after = shifted(edges[0], "hx", -1)
    before = shifted(edges[1], "hx", 1)
    west = shifted(north_message, "hy", 1)
    east = shifted(south_message, "hy", -1)
    section, message = pl.pallas_call(
        section_kernel,
        out_shape=(f32(FIELDS, levels, 16, LANES), f32(parts, levels + 2, 4, LANES)),
        in_specs=[SM, SM] + [VM] * 9,
        out_specs=(VM, VM),
        name="section",
    )(
        first_flux,
        second_flux,
        state,
        scale,
        faces,
        flips,
        west,
        east,
        before,
        after,
        jnp.asarray(weight_table()),
    )
    columns = lax.all_to_all(message, "vz", split_axis=0, concat_axis=0, tiled=True)
    back = pl.pallas_call(
        solve,
        out_shape=f32(parts, levels + 2, 4, LANES),
        in_specs=[VM, VM],
        out_specs=VM,
        name="solve",
    )(factors, columns)
    returned = lax.all_to_all(back, "vz", split_axis=0, concat_axis=0, tiled=True)
    updated = pl.pallas_call(
        finish,
        out_shape=f32(FIELDS, levels, 16, LANES),
        in_specs=[VM, VM],
        out_specs=VM,
        name="finish",
    )(section, returned)
    return updated.reshape(prognostic.shape)


def solution(mesh):
    placed = (
        P(None, "vz", None, None, "hy", "hx"),
        P(None, None, "hy", "hx"),
        P(),
        P(),
        P(None, "hy", "hx"),
        P(None, "hy", "hx"),
        P(None, None, "vz", None, "hy", "hx"),
        P("vz", None, "hy", "hx"),
    )
    return jax.shard_map(
        per_device,
        mesh=mesh,
        in_specs=placed,
        out_specs=P(None, "vz", None, None, "hy", "hx"),
        check_vma=False,
    )
```

time: 186 us -> 103 us (0.55)
  other arithmetic: 46.4 us -> 0.6 us
  waiting for transfers between devices: 41.2 us -> 22.1 us
  local copies, waits for them, and re-layouts: 20.3 us -> 2.84 us
  Pallas kernels: 0 us -> 15.6 us
  matrix products: 9.88 us -> 0 us
  blocking collectives: 24.8 us -> 18.4 us
  starting transfers between devices: 40 us -> 42.5 us
    sub x41 -> x0, other arithmetic: 18.1 us -> none  [the longest x34 14.2 us: solve_unrolled(): scaled[height] - ratios[height] * next_one - seconds[height] * next_two]
    ppermute x4 -> x6, waiting for transfers between devices: 30 us -> 12.1 us  [shifted(): return lax.ppermute(x, axis, [(i, (i + by) % size) for i in range(size)])]
    pallas_call x0 -> x5, Pallas kernels: none -> 15.6 us  [the longest x1 5.13 us: per_device(): pl.pallas_call(section_kernel, out_shape=(f32(FIELDS, levels, 16, LANES),...]
    div x23 -> x0, other arithmetic: 15.2 us -> none  [the longest x21 13.8 us: solve_unrolled(): (source[height] - entry_a[height] * far_value - reduced * near_value) / p...]
    dot_general x6 -> x0, matrix products: 9.88 us -> none  [the longest x1 2.86 us: section_values(): jnp.einsum('cj,fljiab->flciab', derivative, flux_second, precision=highest)]
    slice x20 -> x1, local copies, waits for them, and re-layouts: 9.75 us -> 0.71 us  [per_device(): west_table = shifted(jnp.stack([faces[0], flips[0]]), 'hy', -1)]
    all_to_all x1, blocking collectives: 24.8 us -> 18.4 us  [per_device(): lax.all_to_all(back, 'vz', split_axis=0, concat_axis=0, tiled=True)]
    ppermute x4 -> x6, starting transfers between devices: 24.8 us -> 30.8 us  [shifted(): return lax.ppermute(x, axis, [(i, (i + by) % size) for i in range(size)])]
  transfers between devices with their start and end apart: 5 -> 7, of which waited for: 3 -> 3; matrix products, arithmetic and copies ran while one was open for 12% -> 1% of each run, Pallas kernels for 0% -> 3%
where the time goes in v1:
time: 103 us; the launch traced here: 102 us
  starting transfers between devices  42.5 us (41%)
  waiting for transfers between devices  22.1 us (21%)
  blocking collectives  18.4 us (18%)
  Pallas kernels  15.6 us (15%)
  local copies, waits for them, and re-layouts  2.84 us (3%)
    ppermute x6, starting transfers between devices, shifted(): return lax.ppermute(x, axis, [(i, (i + by) % size) for i in range(size)])  30.8 us
    all_to_all x1, blocking collectives, per_device(): lax.all_to_all(back, 'vz', split_axis=0, concat_axis=0, tiled=True)  18.4 us
    ppermute x6, waiting for transfers between devices, shifted(): return lax.ppermute(x, axis, [(i, (i + by) % size) for i in range(size)])  12.1 us
    all_to_all x1, starting transfers between devices, per_device(): lax.all_to_all(message, 'vz', split_axis=0, concat_axis=0, tiled=True)  11.7 us
    all_to_all x1, waiting for transfers between devices, per_device(): lax.all_to_all(message, 'vz', split_axis=0, concat_axis=0, tiled=True)  9.95 us
    pallas_call x1, Pallas kernels, per_device(): pl.pallas_call(section_kernel, out_shape=(f32(FIELDS, levels, 16, LANES),...  5.13 us
    pallas_call x1, Pallas kernels, per_device(): pl.pallas_call(pack_kernel, out_shape=(f32(FIELDS, levels, 4, LANES), f32...  3.53 us
    pallas_call x1, Pallas kernels, per_device(): pl.pallas_call(factor, out_shape=f32(5, levels * parts // 2, ROWS, LANES)...  2.72 us
  transfers between devices with their start and end apart: 7, of which 3 were waited for; matrix products, arithmetic and copies ran while one was open for 1% of the time, Pallas kernels for 3%

profile of v1, /device:TPU:1, one launch (start us, length us, event | category | flops | bytes accessed | tf_op | source)
XLA Modules:
  0.0 102.1 jit_solution(3055575518849505763)
XLA Ops:
  0.0 0.7 slice_bitcast_fusion.4
  0.7 4.0 %collective-permute-start.1 = (s32[2,128]{1,0:T(2,128)S(1)}, s32[2,128]{1,0:T(2,128)S(1)}, u32[]{:S(2)}, u32[]{:S(2)}) collective-permute-start(s32[2,128]{1,0:T(2,128)S(1)} %pad_add_fusion.2), channel_id=1, source_target_pairs={{0,4},{4,8},{8,12},{12,0},{1,5},{5,9},{9,13},{13,1},{2,6},{6,10},{... | collective-permute-start | bytes 3080 | tf_op jit(solution)/shard_map/ppermute | solution.py:404
  4.8 3.4 %collective-permute-start = (s32[2,128]{1,0:T(2,128)S(1)}, s32[2,128]{1,0:T(2,128)S(1)}, u32[]{:S(2)}, u32[]{:S(2)}) collective-permute-start(s32[2,128]{1,0:T(2,128)S(1)} %pad_add_fusion.1), channel_id=1, source_target_pairs={{0,12},{4,0},{8,4},{12,8},{1,13},{5,1},{9,5},{13,9},{2,14},{6,2},{... | collective-permute-start | bytes 3080 | tf_op jit(solution)/shard_map/ppermute | solution.py:404
  8.1 0.0 collective-permute-done.1
  8.1 0.9 collective-permute-done
  9.1 0.6 pad_add_fusion.tables
  9.7 3.5 %pack.1 = (f32[5,20,4,128]{3,2,1,0:T(4,128)}, f32[5,20,4,128]{3,2,1,0:T(4,128)}, f32[2,16,128]{2,1,0:T(8,128)}) custom-call(f32[5,20,16,128]{3,2,1,0:T(8,128)} %bitcast.21, s32[4,128]{1,0:T(4,128)} %pad_add_fusion.tables), custom_call_target="tpu_custom_call" | custom-call | tf_op jit(solution)/shard_map/pack/pallas_call | solution.py:417
  13.2 3.2 %collective-permute-start.2 = (f32[5,20,4,128]{3,2,1,0:T(4,128)}, f32[5,20,4,128]{3,2,1,0:T(4,128)S(1)}, u32[]{:S(2)}, u32[]{:S(2)}) collective-permute-start(f32[5,20,4,128]{3,2,1,0:T(4,128)} %get-tuple-element.10), channel_id=1, source_target_pairs={{0,4},{4,8},{8,12},{12,0},{1,5},{5,9},{9,13},{13,1},{2,6},{6,10},{... | collective-permute-start | bytes 614408 | tf_op jit(solution)/shard_map/ppermute | solution.py:404
  16.4 3.3 %collective-permute-start.3 = (f32[5,20,4,128]{3,2,1,0:T(4,128)}, f32[5,20,4,128]{3,2,1,0:T(4,128)S(1)}, u32[]{:S(2)}, u32[]{:S(2)}) collective-permute-start(f32[5,20,4,128]{3,2,1,0:T(4,128)} %get-tuple-element.11), channel_id=1, source_target_pairs={{0,12},{4,0},{8,4},{12,8},{1,13},{5,1},{9,5},{13,9},{2,14},{6,2},{... | collective-permute-start | bytes 614408 | tf_op jit(solution)/shard_map/ppermute | solution.py:404
  19.7 0.7 slice_bitcast_fusion
  20.4 15.1 %collective-permute-start.5 = (f32[16,128]{1,0:T(8,128)S(1)}, f32[16,128]{1,0:T(8,128)S(1)}, u32[]{:S(2)}, u32[]{:S(2)}) collective-permute-start(f32[16,128]{1,0:T(8,128)S(1)} %get-tuple-element.15), channel_id=1, source_target_pairs={{0,496},{16,0},{32,16},{48,32},{64,48},{80,64},{96,80},{112,96},{1... | collective-permute-start | bytes 24584 | tf_op jit(solution)/shard_map/ppermute | solution.py:404
  35.5 1.9 %collective-permute-start.4 = (f32[16,128]{1,0:T(8,128)S(1)}, f32[16,128]{1,0:T(8,128)S(1)}, u32[]{:S(2)}, u32[]{:S(2)}) collective-permute-start(f32[16,128]{1,0:T(8,128)S(1)} %get-tuple-element.16), channel_id=1, source_target_pairs={{0,16},{16,32},{32,48},{48,64},{64,80},{80,96},{96,112},{112,128},... | collective-permute-start | bytes 24584 | tf_op jit(solution)/shard_map/ppermute | solution.py:404
  37.4 0.0 collective-permute-done.5.after
  37.4 0.0 copy-start.3
  37.4 11.2 %collective-permute-done.4.before = f32[16,128]{1,0:T(8,128)S(1)} collective-permute-done((f32[16,128]{1,0:T(8,128)S(1)}, f32[16,128]{1,0:T(8,128)S(1)}, u32[]{:S(2)}, u32[]{:S(2)}) %collective-permute-start.4) | collective-permute-done | bytes 8224 | tf_op jit(solution)/shard_map/ppermute | solution.py:404
  48.6 0.0 copy-start.4
  48.6 0.0 collective-permute-done.2.west
  48.6 0.0 copy-start.1
  48.6 0.0 collective-permute-done.3.east
  48.6 0.0 copy-start.2
  48.6 0.0 copy-done.3
  48.6 0.6 copy-done.4
  49.2 0.1 copy-done.1
  49.3 0.1 copy-done.2
  49.3 5.1 %section.1 = (f32[5,20,16,128]{3,2,1,0:T(8,128)}, f32[4,22,4,128]{3,2,1,0:T(4,128)}) custom-call(f32[5,5]{1,0:T(8,128)} %first.1, f32[5,5]{1,0:T(8,128)} %second.1, f32[5,20,16,128]{3,2,1,0:T(8,128)} %bitcast.22, f32[16,128]{1,0:T(8,128)} %bitcast.24, s32[4,128]{1,0:T(4,128)} %bitcast.25, s32[4,128]{1,0:T(4,128)} %bitcast.26, f32[5,20,4,128]{3,2,1,0:T(4,128)} %copy-done.1, ...), custom_call_target="tpu_custom_call" | custom-call | tf_op jit(solution)/shard_map/section/pallas_call | solution.py:428
  54.5 11.7 %all-to-all-start = ((f32[4,22,4,128]{3,2,1,0:T(4,128)}), f32[4,22,4,128]{3,2,1,0:T(4,128)S(1)}, u32[]{:S(2)}, u32[]{:S(2)}) async-start(f32[4,22,4,128]{3,2,1,0:T(4,128)} %get-tuple-element.14), calls=%async_computation | async-start | bytes 360448 | tf_op jit(solution)/shard_map/all_to_all | solution.py:447
  66.1 2.7 %factor.1.factors = f32[5,40,8,128]{3,2,1,0:T(8,128)} custom-call(f32[4,80,4,128]{3,2,1,0:T(4,128)} %bitcast.23, f32[4,128]{1,0:T(4,128)} %bitcast.27), custom_call_target="tpu_custom_call" | custom-call | flops 4000000 | bytes 1500000 | tf_op jit(solution)/shard_map/factor/pallas_call | solution.py:409
  68.9 10.0 %all-to-all-done.columns = f32[4,22,4,128]{3,2,1,0:T(4,128)S(1)} async-done(((f32[4,22,4,128]{3,2,1,0:T(4,128)}), f32[4,22,4,128]{3,2,1,0:T(4,128)S(1)}, u32[]{:S(2)}, u32[]{:S(2)}) %all-to-all-start) | async-done | bytes 180256 | tf_op jit(solution)/shard_map/all_to_all | solution.py:447
  78.8 0.0 copy-start
  78.8 0.7 copy-done
  79.5 2.0 %solve.1 = f32[4,22,4,128]{3,2,1,0:T(4,128)} custom-call(f32[5,40,8,128]{3,2,1,0:T(8,128)} %factor.1.factors, f32[4,22,4,128]{3,2,1,0:T(4,128)} %copy-done), custom_call_target="tpu_custom_call" | custom-call | tf_op jit(solution)/shard_map/solve/pallas_call | solution.py:448
  81.5 18.4 %all_to_all.10.returned = f32[4,22,4,128]{3,2,1,0:T(4,128)} all-to-all(f32[4,22,4,128]{3,2,1,0:T(4,128)} %solve.1), channel_id=1, replica_groups=mesh['hx'=32,'hy'=4,'vz'=4] {'vz'}, dimensions={0} | all-to-all | bytes 360448 | tf_op jit(solution)/shard_map/all_to_all | solution.py:455
  99.9 2.2 %finish.1 = f32[5,20,16,128]{3,2,1,0:T(8,128)} custom-call(f32[5,20,16,128]{3,2,1,0:T(8,128)} %get-tuple-element.13.section, f32[4,22,4,128]{3,2,1,0:T(4,128)} %all_to_all.10.returned), custom_call_target="tpu_custom_call" | custom-call | tf_op jit(solution)/shard_map/finish/pallas_call | solution.py:456
  (2 shorter events, 0.0 us)
Async XLA Ops:
  0.7 7.4 %collective-permute-start.1 = (s32[2,128]{1,0:T(2,128)S(1)}, s32[2,128]{1,0:T(2,128)S(1)}, u32[]{:S(2)}, u32[]{:S(2)}) collective-permute-start(s32[2,128]{1,0:T(2,128)S(1)} %pad_add_fusion.2), channel_id=1, source_target_pairs={{0,4},{4,8},{8,12},{12,0},{1,5},{5,9},{9,13},{13,1},{2,6},{6,10},{... | collective-permute-start | bytes 3080 | tf_op jit(solution)/shard_map/ppermute | solution.py:404
  4.8 4.3 %collective-permute-start = (s32[2,128]{1,0:T(2,128)S(1)}, s32[2,128]{1,0:T(2,128)S(1)}, u32[]{:S(2)}, u32[]{:S(2)}) collective-permute-start(s32[2,128]{1,0:T(2,128)S(1)} %pad_add_fusion.1), channel_id=1, source_target_pairs={{0,12},{4,0},{8,4},{12,8},{1,13},{5,1},{9,5},{13,9},{2,14},{6,2},{... | collective-permute-start | bytes 3080 | tf_op jit(solution)/shard_map/ppermute | solution.py:404
  13.2 35.4 %collective-permute-start.2 = (f32[5,20,4,128]{3,2,1,0:T(4,128)}, f32[5,20,4,128]{3,2,1,0:T(4,128)S(1)}, u32[]{:S(2)}, u32[]{:S(2)}) collective-permute-start(f32[5,20,4,128]{3,2,1,0:T(4,128)} %get-tuple-element.10), channel_id=1, source_target_pairs={{0,4},{4,8},{8,12},{12,0},{1,5},{5,9},{9,13},{13,1},{2,6},{6,10},{... | collective-permute-start | bytes 614408 | tf_op jit(solution)/shard_map/ppermute | solution.py:404
  16.4 32.2 %collective-permute-start.3 = (f32[5,20,4,128]{3,2,1,0:T(4,128)}, f32[5,20,4,128]{3,2,1,0:T(4,128)S(1)}, u32[]{:S(2)}, u32[]{:S(2)}) collective-permute-start(f32[5,20,4,128]{3,2,1,0:T(4,128)} %get-tuple-element.11), channel_id=1, source_target_pairs={{0,12},{4,0},{8,4},{12,8},{1,13},{5,1},{9,5},{13,9},{2,14},{6,2},{... | collective-permute-start | bytes 614408 | tf_op jit(solution)/shard_map/ppermute | solution.py:404
  20.4 17.0 %collective-permute-start.5 = (f32[16,128]{1,0:T(8,128)S(1)}, f32[16,128]{1,0:T(8,128)S(1)}, u32[]{:S(2)}, u32[]{:S(2)}) collective-permute-start(f32[16,128]{1,0:T(8,128)S(1)} %get-tuple-element.15), channel_id=1, source_target_pairs={{0,496},{16,0},{32,16},{48,32},{64,48},{80,64},{96,80},{112,96},{1... | collective-permute-start | bytes 24584 | tf_op jit(solution)/shard_map/ppermute | solution.py:404
  35.5 13.1 %collective-permute-start.4 = (f32[16,128]{1,0:T(8,128)S(1)}, f32[16,128]{1,0:T(8,128)S(1)}, u32[]{:S(2)}, u32[]{:S(2)}) collective-permute-start(f32[16,128]{1,0:T(8,128)S(1)} %get-tuple-element.16), channel_id=1, source_target_pairs={{0,16},{16,32},{32,48},{48,64},{64,80},{80,96},{96,112},{112,128},... | collective-permute-start | bytes 24584 | tf_op jit(solution)/shard_map/ppermute | solution.py:404
  37.4 11.2 %copy-start.3 = (f32[16,128]{1,0:T(8,128)}, f32[16,128]{1,0:T(8,128)S(1)}, u32[]{:S(2)}) copy-start(f32[16,128]{1,0:T(8,128)S(1)} %collective-permute-done.5.after) | copy-start | bytes 24580
  48.6 0.6 copy-start.4
  48.6 0.7 copy-start.1
  48.6 0.7 copy-start.2
  54.5 24.3 %all-to-all-start = ((f32[4,22,4,128]{3,2,1,0:T(4,128)}), f32[4,22,4,128]{3,2,1,0:T(4,128)S(1)}, u32[]{:S(2)}, u32[]{:S(2)}) async-start(f32[4,22,4,128]{3,2,1,0:T(4,128)} %get-tuple-element.14), calls=%async_computation | async-start | bytes 360448 | tf_op jit(solution)/shard_map/all_to_all | solution.py:447
  78.8 0.7 copy-start

commit v2 on v1

--- a/solution.py
+++ b/solution.py
@@ -356,20 +356,102 @@
 
 VM = pl.BlockSpec(memory_space=pltpu.VMEM)
 SM = pl.BlockSpec(memory_space=pltpu.SMEM)
+MESH = pl.DeviceIdType.MESH
 
 
 def f32(*shape):
     return jax.ShapeDtypeStruct(shape, jnp.float32)
 
 
-def pack_kernel(state, tables, north_message, south_message, edges):
-    pack_faces(state, tables[...], north_message, south_message)
+def whole_kernel(
+    sizes,
+    first,
+    second,
+    state,
+    scale,
+    faces,
+    flips,
+    coupling,
+    damping,
+    weights,
+    section,
+    returned,
+    tables,
+    north_message,
+    south_message,
+    edges,
+    west,
+    east,
+    before,
+    after,
+    factors,
+    message,
+    columns,
+    back,
+    send_sem,
+    recv_sem,
+):
+    hx, hy, vz = (lax.axis_index(axis) for axis in ("hx", "hy", "vz"))
+    size_x, size_y, parts = sizes
+
+    def place(dx=0, dy=0, dz=0):
+        return (
+            lax.rem(hx + dx + size_x, size_x),
+            lax.rem(hy + dy + size_y, size_y),
+            lax.rem(vz + dz, parts),
+        )
+
+    partners = [place(dx=1), place(dx=-1), place(dy=1), place(dy=-1)]
+    partners += [place(dz=d) for d in range(1, parts)]
+    barrier = pltpu.get_barrier_semaphore()
+    for partner in partners:
+        pl.semaphore_signal(barrier, inc=1, device_id=partner, device_id_type=MESH)
+
+    def copy(number, source, target, device):
+        return pltpu.make_async_remote_copy(
+            src_ref=source,
+            dst_ref=target,
+            send_sem=send_sem.at[number],
+            recv_sem=recv_sem.at[number],
+            device_id=device,
+            device_id_type=MESH,
+        )
+
     pack_edges(state, edges)
-
-
-def section_kernel(
-    first, second, state, scale, faces, flips, west, east, before, after, weights, section, message
-):
+    pl.semaphore_wait(barrier, len(partners))
+    to_tables = [
+        copy(0, faces, tables.at[0], place(dy=-1)),
+        copy(1, flips, tables.at[1], place(dy=-1)),
+        copy(2, faces, tables.at[2], place(dy=1)),
+        copy(3, flips, tables.at[3], place(dy=1)),
+    ]
+    for each in to_tables:
+        each.start()
+    to_edges = [
+        copy(4, edges.at[0], after, place(dx=-1)),
+        copy(5, edges.at[1], before, place(dx=1)),
+    ]
+    for each in to_edges:
+        each.start()
+    for each in to_tables:
+        each.wait_recv()
+    pack_faces(
+        state,
+        jnp.concatenate(
+            [tables[0, 0:1], tables[1, 0:1], tables[2, 1:2], tables[3, 1:2]], axis=0
+        ),
+        north_message,
+        south_message,
+    )
+    to_faces = [
+        copy(6, north_message, west, place(dy=1)),
+        copy(7, south_message, east, place(dy=-1)),
+    ]
+    for each in to_faces:
+        each.start()
+    factor(coupling, damping, factors)
+    for each in to_edges + to_faces:
+        each.wait_recv()
     make_section(
         state,
         scale,
@@ -385,52 +467,72 @@
         section,
     )
     column_message(section, message)
+    to_columns = []
+    for d in range(1, parts):
+        peer = place(dz=d)
+        to_columns.append(copy(7 + d, message.at[peer[2]], columns.at[vz], peer))
+        to_columns[-1].start()
+    columns[vz] = message[vz]
+    for each in to_columns:
+        each.wait_recv()
+    solve(factors, columns, back)
+    to_back = []
+    for d in range(1, parts):
+        peer = place(dz=d)
+        to_back.append(copy(6 + parts + d, back.at[peer[2]], returned.at[vz], peer))
+        to_back[-1].start()
+    returned[vz] = back[vz]
+    for each in to_back:
+        each.wait_recv()
+    for each in to_tables + to_edges + to_faces + to_columns + to_back:
+        each.wait_send()
 
 
 def per_device(
-    prognostic, metric, first_flux, second_flux, neighbour_face, orientation, coupling, damping
+    sizes,
+    prognostic,
+    metric,
+    first_flux,
+    second_flux,
+    neighbour_face,
+    orientation,
+    coupling,
+    damping,
 ):
     levels = prognostic.shape[1]
-    parts = lax.axis_size("vz")
+    parts = sizes[2]
     state = prognostic.reshape(FIELDS, levels, 16, LANES)
     scale = metric.reshape(16, LANES)
     faces = neighbour_face.reshape(4, LANES)
     flips = orientation.reshape(4, LANES)
     couples = coupling.reshape(4, levels * parts, 4, LANES)
     damp = damping.reshape(4, LANES)
-
-    def shifted(x, axis, by):
-        size = lax.axis_size(axis)
-        return lax.ppermute(x, axis, [(i, (i + by) % size) for i in range(size)])
-
-    west_table = shifted(jnp.stack([faces[0], flips[0]]), "hy", -1)
-    east_table = shifted(jnp.stack([faces[1], flips[1]]), "hy", 1)
-    tables = jnp.concatenate([west_table, east_table])
-    factors = pl.pallas_call(
-        factor,
-        out_shape=f32(5, levels * parts // 2, ROWS, LANES),
-        in_specs=[VM, VM],
-        out_specs=VM,
-        name="factor",
-        cost_estimate=pl.CostEstimate(flops=4000000, bytes_accessed=1500000, transcendentals=0),
-    )(couples, damp)
-    north_message, south_message, edges = pl.pallas_call(
-        pack_kernel,
-        out_shape=(f32(FIELDS, levels, 4, LANES), f32(FIELDS, levels, 4, LANES), f32(2, 16, LANES)),
-        in_specs=[VM, VM],
-        out_specs=(VM, VM, VM),
-        name="pack",
-    )(state, tables)
-    after = shifted(edges[0], "hx", -1)
-    before = shifted(edges[1], "hx", 1)
-    west = shifted(north_message, "hy", 1)
-    east = shifted(south_message, "hy", -1)
-    section, message = pl.pallas_call(
-        section_kernel,
+    copies = 6 + 2 * parts
+    trace = pltpu.VMEM((FIELDS, levels, 4, LANES), jnp.float32)
+    column = pltpu.VMEM((parts, levels + 2, 4, LANES), jnp.float32)
+    section, returned = pl.pallas_call(
+        functools.partial(whole_kernel, sizes),
         out_shape=(f32(FIELDS, levels, 16, LANES), f32(parts, levels + 2, 4, LANES)),
-        in_specs=[SM, SM] + [VM] * 9,
+        in_specs=[SM, SM] + [VM] * 7,
         out_specs=(VM, VM),
-        name="section",
+        scratch_shapes=[
+            pltpu.VMEM((4, 4, LANES), jnp.int32),
+            trace,
+            trace,
+            pltpu.VMEM((2, 16, LANES), jnp.float32),
+            trace,
+            trace,
+            pltpu.VMEM((16, LANES), jnp.float32),
+            pltpu.VMEM((16, LANES), jnp.float32),
+            pltpu.VMEM((5, levels * parts // 2, ROWS, LANES), jnp.float32),
+            column,
+            column,
+            column,
+            pltpu.SemaphoreType.DMA((copies,)),
+            pltpu.SemaphoreType.DMA((copies,)),
+        ],
+        compiler_params=pltpu.CompilerParams(collective_id=0, has_side_effects=True),
+        name="exchange",
     )(
         first_flux,
         second_flux,
@@ -438,21 +540,10 @@
         scale,
         faces,
         flips,
-        west,
-        east,
-        before,
-        after,
+        couples,
+        damp,
         jnp.asarray(weight_table()),
     )
-    columns = lax.all_to_all(message, "vz", split_axis=0, concat_axis=0, tiled=True)
-    back = pl.pallas_call(
-        solve,
-        out_shape=f32(parts, levels + 2, 4, LANES),
-        in_specs=[VM, VM],
-        out_specs=VM,
-        name="solve",
-    )(factors, columns)
-    returned = lax.all_to_all(back, "vz", split_axis=0, concat_axis=0, tiled=True)
     updated = pl.pallas_call(
         finish,
         out_shape=f32(FIELDS, levels, 16, LANES),
@@ -474,8 +565,9 @@
         P(None, None, "vz", None, "hy", "hx"),
         P("vz", None, "hy", "hx"),
     )
+    sizes = (mesh.shape["hx"], mesh.shape["hy"], mesh.shape["vz"])
     return jax.shard_map(
-        per_device,
+        functools.partial(per_device, sizes),
         mesh=mesh,
         in_specs=placed,
         out_specs=P(None, "vz", None, None, "hy", "hx"),

time: 103 us -> 57 us (0.55)
  starting transfers between devices: 42.5 us -> 0 us
  Pallas kernels: 15.6 us -> 56.8 us
  waiting for transfers between devices: 22.1 us -> 0 us
  blocking collectives: 18.4 us -> 0 us
  local copies, waits for them, and re-layouts: 2.84 us -> 0 us
    pallas_call x4 -> x1, Pallas kernels: 13.4 us -> 54.6 us  [per_device(): pl.pallas_call(functools.partial(whole_kernel, sizes), out_shape=(f32(FIE...]
    ppermute x6 -> x0, starting transfers between devices: 30.8 us -> none  [shifted(): return lax.ppermute(x, axis, [(i, (i + by) % size) for i in range(size)])]
    all_to_all x1 -> x0, blocking collectives: 18.4 us -> none  [per_device(): lax.all_to_all(back, 'vz', split_axis=0, concat_axis=0, tiled=True)]
    ppermute x6 -> x0, waiting for transfers between devices: 12.1 us -> none  [shifted(): return lax.ppermute(x, axis, [(i, (i + by) % size) for i in range(size)])]
    all_to_all x1 -> x0, starting transfers between devices: 11.7 us -> none  [per_device(): lax.all_to_all(message, 'vz', split_axis=0, concat_axis=0, tiled=True)]
    all_to_all x1 -> x0, waiting for transfers between devices: 9.95 us -> none  [per_device(): lax.all_to_all(message, 'vz', split_axis=0, concat_axis=0, tiled=True)]
    unnamed x10 -> x0, local copies, waits for them, and re-layouts: 1.42 us -> none
  transfers between devices with their start and end apart: 7 -> 0, of which waited for: 3 -> 0; matrix products, arithmetic and copies ran while one was open for 1% -> 0% of each run, Pallas kernels for 3% -> 0%
where the time goes in v2:
time: 57 us; the launch traced here: 56.8 us
  Pallas kernels  56.8 us (100%)
    pallas_call x1, Pallas kernels, per_device(): pl.pallas_call(functools.partial(whole_kernel, sizes), out_shape=(f32(FIE...  54.6 us
    pallas_call x1, Pallas kernels, per_device(): pl.pallas_call(finish, out_shape=f32(FIELDS, levels, 16, LANES), in_specs...  2.19 us

profile of v2, /device:TPU:1, one launch (start us, length us, event | category | flops | bytes accessed | tf_op | source)
XLA Modules:
  0.0 56.8 jit_solution(10482769035477946811)
XLA Ops:
  0.0 54.6 %exchange.1 = (f32[5,20,16,128]{3,2,1,0:T(8,128)}, f32[4,22,4,128]{3,2,1,0:T(4,128)}) custom-call(f32[5,5]{1,0:T(8,128)} %first.1, f32[5,5]{1,0:T(8,128)} %second.1, f32[5,20,16,128]{3,2,1,0:T(8,128)} %bitcast.9, f32[16,128]{1,0:T(8,128)} %bitcast.11, s32[4,128]{1,0:T(4,128)} %bitcast.12, s32[4,128]{1,0:T(4,128)} %bitcast.13, f32[4,80,4,128]{3,2,1,0:T(4,128)} %bitcast.10, ...), custom_call_target="tpu_custom_call" | custom-call | tf_op jit(solution)/shard_map/exchange/pallas_call | solution.py:513
  54.6 2.2 %finish.1 = f32[5,20,16,128]{3,2,1,0:T(8,128)} custom-call(f32[5,20,16,128]{3,2,1,0:T(8,128)} %get-tuple-element.7.section, f32[4,22,4,128]{3,2,1,0:T(4,128)} %get-tuple-element.8.returned), custom_call_target="tpu_custom_call" | custom-call | tf_op jit(solution)/shard_map/finish/pallas_call | solution.py:547

commit v3 on v2

--- a/solution.py
+++ b/solution.py
@@ -168,7 +168,7 @@
 
 
 def make_section(
-    state, scale, first, second, faces, flips, west, east, before, after, weights, section
+    state, scale, first, second, faces, flips, sides, before, after, weights, section, targets
 ):
     levels = state.shape[1]
     row, lane = rows_of(), lanes_of()
@@ -181,8 +181,7 @@
     )
     edge = edge_values(before, after, faces, flips)
     at_edge = ((row < 4) & (lane == 0)) | ((row >= 4) & (lane == LANES - 1))
-    left = row % 4 < 2
-    place = [jnp.where(left, 2 * tile + row // 4, 4 + 2 * tile + row // 4) for tile in range(2)]
+    place = side_rows()
 
     def at(count, carry):
         q1 = [[None] * 2 for _ in range(FIELDS)]
@@ -197,23 +196,28 @@
             across = halves(pltpu.roll(chosen, 1, 1), pltpu.roll(chosen, LANES - 1, 1))
             shift = lax.rem(2 * LANES - number, LANES)
             across = jnp.where(at_edge, pltpu.roll(edge, shift, 1), across)
-            sides = jnp.concatenate([west[field, count], east[field, count]], axis=0)
+            if sides is not None:
+                beside = pair(sides[0][field, count], sides[1][field, count])
             for t in range(2):
-                along = take_rows(sides, place[t])
-                total = weights[3] * tiles[t] - weights[15] * along
+                total = weights[3] * tiles[t]
                 for offset in (-3, -2, -1, 1, 2, 3):
                     total += weights[offset + 3] * pltpu.roll(tiles[t], (-offset) % ROWS, 0)
+                if sides is not None:
+                    along = take_rows(beside, place[t])
+                    total -= weights[15] * along
                 q1[field][t] = total
                 total = -weights[17 + t] * across
                 for other in range(2):
                     total += weights[7 + 4 * t + 2 * other] * tiles[other]
                     total += weights[8 + 4 * t + 2 * other] * swapped[other]
                 q2[field][t] = total
-                rest[field][t] = (
-                    weights[21 + t] * tiles[t] + weights[16] * along + weights[19 + t] * across
-                )
-                own[field][t] = tiles[t]
-        for field in range(FIELDS):
+                if field in targets:
+                    total = weights[21 + t] * tiles[t] + weights[19 + t] * across
+                    if sides is not None:
+                        total += weights[16] * along
+                    rest[field][t] = total
+                    own[field][t] = tiles[t]
+        for field in targets:
             for t in range(2):
                 total = rest[field][t]
                 for other in range(FIELDS):
@@ -227,7 +231,57 @@
     lax.fori_loop(0, levels, at, 0)
 
 
-def column_message(section, message):
+def side_rows():
+    row = rows_of()
+    left = row % 4 < 2
+    return [jnp.where(left, 2 * tile + row // 4, 4 + 2 * tile + row // 4) for tile in range(2)]
+
+
+def add_sides(scale, first, sides, weights, section, targets):
+    levels = section.shape[1]
+    place = side_rows()
+
+    def at(count, carry):
+        beside = [pair(sides[0][g, count], sides[1][g, count]) for g in range(FIELDS)]
+        for t in range(2):
+            span = slice(t * ROWS, (t + 1) * ROWS)
+            along = [take_rows(each, place[t]) for each in beside]
+            for field in targets:
+                total = first[field, 0] * along[0]
+                for other in range(1, FIELDS):
+                    total += first[field, other] * along[other]
+                total = weights[16] * along[field] - weights[15] * total
+                section[field, count, span] += step_size * scale[span] * total
+        return carry
+
+    lax.fori_loop(0, levels, at, 0, unroll=2)
+
+
+def point_pair(part):
+    return (1, 2) if part == 0 else (0, 3)
+
+
+def gathered(entries, base, part):
+    row = rows_of()
+    low, high = point_pair(part)
+    total = None
+    for m in range(4):
+        if entries[m] is None:
+            continue
+        index = jnp.where(row % 2 == 0, base[m] + low, base[m] + high)
+        moved = take_rows(entries[m], index)
+        total = moved if total is None else jnp.where(row // 2 == m, moved, total)
+    for m in range(4):
+        if entries[m] is None:
+            total = jnp.where(row // 2 == m, 0.0, total)
+    return total
+
+
+def scattered(tile, m):
+    return take_rows(tile, 2 * m + (rows_of() % 4) // 2)
+
+
+def column_message(section, message, part):
     levels = section.shape[1]
     for t in range(2):
         span = slice(t * ROWS, (t + 1) * ROWS)
@@ -241,9 +295,12 @@
                 total = total + gravity_couple * warm[count - 1]
             entries.append(total)
         entries += [warm[0], warm[levels - 1]]
-        for count, entry in enumerate(entries):
-            message[2 * t, count] = entry[0:4]
-            message[2 * t + 1, count] = entry[4:8]
+        entries += [None] * (-len(entries) % 4)
+        for p in range(len(entries) // 4):
+            for side in range(2):
+                message[2 * t + side, p] = gathered(
+                    entries[4 * p : 4 * p + 4], [4 * side] * 4, part
+                )
 
 
 def pair(low, high):
@@ -279,83 +336,89 @@
     lax.fori_loop(0, half, at, (zero,) * 4)
 
 
-def solve(factors, columns, message):
-    parts, count = columns.shape[0], columns.shape[1] - 2
+def solve(factors, columns, message, part, count):
+    parts = columns.shape[0]
     levels = parts * count
     half = levels // 2
 
+    def entry_of(d, place):
+        return scattered(columns[d, place // 4], place % 4)
+
     def source(level):
         d, place = level // count, level % count
-        entry = columns[d, place]
+        entry = entry_of(d, place)
         if place == 0 and d > 0:
-            entry = entry + gravity_couple * columns[d - 1, count + 1]
+            entry = entry + gravity_couple * entry_of(d - 1, count + 1)
         if place == count - 1 and d < parts - 1:
-            entry = entry - gravity_couple * columns[d + 1, count]
+            entry = entry - gravity_couple * entry_of(d + 1, count)
         return entry
 
     far = near = jnp.zeros((ROWS, LANES), jnp.float32)
     scaled = []
     for t in range(half):
-        entry = pair(source(t), source(levels - 1 - t)) * factors[0, t]
+        entry = halves(source(t), source(levels - 1 - t)) * factors[0, t]
         far, near = near, (entry + factors[1, t] * far) - factors[2, t] * near
         scaled.append(near)
     top, under = half - 1, half - 2
-    value_1, value_2 = scaled[top], scaled[under]
     ratio_1, ratio_2 = factors[3, top], factors[3, under]
     second_1, second_2 = factors[4, top], factors[4, under]
-    other_value = pltpu.roll(value_2, 4, 0)
-    other_ratio = pltpu.roll(ratio_2, 4, 0)
-    other_second = pltpu.roll(second_2, 4, 0)
-    here = 1.0 - second_1 * other_second
-    there = ratio_1 - second_1 * other_ratio
-    right = value_1 - second_1 * other_value
+    here = 1.0 - second_1 * pltpu.roll(second_2, 4, 0)
+    there = ratio_1 - second_1 * pltpu.roll(ratio_2, 4, 0)
+    right = scaled[top] - second_1 * pltpu.roll(scaled[under], 4, 0)
     here_2 = pltpu.roll(here, 4, 0)
     there_2 = pltpu.roll(there, 4, 0)
     right_2 = pltpu.roll(right, 4, 0)
     mine = (right * here_2 - there * right_2) / (here * here_2 - there * there_2)
     next_one, next_two = mine, pltpu.roll(mine, 4, 0)
-    blank = jnp.zeros((4, LANES), jnp.float32)
-
-    def put(level, entry):
-        for d in range(parts):
-            place = level - d * count + 1
-            if 0 <= place < count + 2:
-                message[d, place] = entry
-
-    put(-1, blank)
-    put(levels, blank)
-    put(top, mine[0:4])
-    put(levels - 1 - top, mine[4:8])
+    found = [None] * half
+    found[top] = mine
     for t in range(half - 2, -1, -1):
-        found = (scaled[t] - factors[4, t] * next_two) - factors[3, t] * next_one
-        put(t, found[0:4])
-        put(levels - 1 - t, found[4:8])
-        next_one, next_two = found, next_one
+        found[t] = (scaled[t] - factors[4, t] * next_two) - factors[3, t] * next_one
+        next_one, next_two = found[t], next_one
+    for d in range(parts):
+        for p in range((count + 2 + 3) // 4):
+            entries, base = [], []
+            for m in range(4):
+                level = d * count - 1 + 4 * p + m
+                inside = 0 <= level < levels and 4 * p + m < count + 2
+                low = level < half
+                entries.append((found[level] if low else found[levels - 1 - level]) if inside else None)
+                base.append(0 if low else 4)
+            message[d, p] = gathered(entries, base, part)
 
 
 def finish(section, returned, updated):
     levels = section.shape[1]
-
-    def at(count, carry):
-        for t in range(2):
-            span = slice(t * ROWS, (t + 1) * ROWS)
-
-            def level(place):
-                return pair(returned[2 * t, place], returned[2 * t + 1, place])
-
-            jump = level(count + 2) - level(count)
+    point = rows_of() % 4
+    inner = (point == 1) | (point == 2)
+    for t in range(2):
+        span = slice(t * ROWS, (t + 1) * ROWS)
+
+        def level(place):
+            p, m = place // 4, place % 4
+            both = [
+                jnp.where(
+                    inner,
+                    scattered(returned[0, 2 * t + side, p], m),
+                    scattered(returned[1, 2 * t + side, p], m),
+                )
+                for side in range(2)
+            ]
+            return halves(both[0], both[1])
+
+        speeds = [level(place) for place in range(levels + 2)]
+        for count in range(levels):
+            jump = speeds[count + 2] - speeds[count]
             updated[0, count, span] = section[0, count, span] - density_couple * jump
             updated[1, count, span] = section[1, count, span]
             updated[2, count, span] = section[2, count, span]
-            updated[3, count, span] = level(count + 1)
+            updated[3, count, span] = speeds[count + 1]
             updated[4, count, span] = section[4, count, span] - theta_couple * jump
-        return carry
-
-    lax.fori_loop(0, levels, at, 0, unroll=2)
 
 
 VM = pl.BlockSpec(memory_space=pltpu.VMEM)
 SM = pl.BlockSpec(memory_space=pltpu.SMEM)
+ANY = pl.BlockSpec(memory_space=pl.ANY)
 MESH = pl.DeviceIdType.MESH
 
 
@@ -367,15 +430,17 @@
     sizes,
     first,
     second,
-    state,
+    state_in,
     scale,
     faces,
     flips,
-    coupling,
+    coupling_in,
     damping,
     weights,
     section,
     returned,
+    state,
+    coupling,
     tables,
     north_message,
     south_message,
@@ -390,6 +455,7 @@
     back,
     send_sem,
     recv_sem,
+    load_sem,
 ):
     hx, hy, vz = (lax.axis_index(axis) for axis in ("hx", "hy", "vz"))
     size_x, size_y, parts = sizes
@@ -417,7 +483,10 @@
             device_id_type=MESH,
         )
 
-    pack_edges(state, edges)
+    load_state = pltpu.make_async_copy(state_in, state, load_sem.at[0])
+    load_coupling = pltpu.make_async_copy(coupling_in, coupling, load_sem.at[1])
+    load_state.start()
+    load_coupling.start()
     pl.semaphore_wait(barrier, len(partners))
     to_tables = [
         copy(0, faces, tables.at[0], place(dy=-1)),
@@ -427,6 +496,8 @@
     ]
     for each in to_tables:
         each.start()
+    load_state.wait()
+    pack_edges(state, edges)
     to_edges = [
         copy(4, edges.at[0], after, place(dx=-1)),
         copy(5, edges.at[1], before, place(dx=1)),
@@ -449,42 +520,59 @@
     ]
     for each in to_faces:
         each.start()
+    for each in to_edges:
+        each.wait_recv()
+
+    def sections(sides, targets):
+        make_section(
+            state,
+            scale,
+            first,
+            second,
+            faces[...],
+            flips[...],
+            sides,
+            before[...],
+            after[...],
+            weights,
+            section,
+            targets,
+        )
+
+    def spread_out(part, base, source, target):
+        sent = []
+        for d in range(1, parts):
+            peer = place(dz=d)
+            number = base + part * (parts - 1) + d - 1
+            sent.append(copy(number, source.at[part, peer[2]], target.at[part, vz], peer))
+            sent[-1].start()
+        target[part, vz] = source[part, vz]
+        return sent
+
+    first_out, first_back = 8, 8 + 2 * (parts - 1)
+    count = state.shape[1]
+    sections(None, (3, 4))
+    column_message(section, message.at[0], 0)
+    out_0 = spread_out(0, first_out, message, columns)
+    for each in to_faces:
+        each.wait_recv()
+    add_sides(scale, first, (west, east), weights, section, (3, 4))
+    column_message(section, message.at[1], 1)
+    out_1 = spread_out(1, first_out, message, columns)
+    load_coupling.wait()
     factor(coupling, damping, factors)
-    for each in to_edges + to_faces:
+    for each in out_0:
         each.wait_recv()
-    make_section(
-        state,
-        scale,
-        first,
-        second,
-        faces[...],
-        flips[...],
-        west,
-        east,
-        before[...],
-        after[...],
-        weights,
-        section,
-    )
-    column_message(section, message)
-    to_columns = []
-    for d in range(1, parts):
-        peer = place(dz=d)
-        to_columns.append(copy(7 + d, message.at[peer[2]], columns.at[vz], peer))
-        to_columns[-1].start()
-    columns[vz] = message[vz]
-    for each in to_columns:
+    solve(factors, columns.at[0], back.at[0], 0, count)
+    back_0 = spread_out(0, first_back, back, returned)
+    for each in out_1:
         each.wait_recv()
-    solve(factors, columns, back)
-    to_back = []
-    for d in range(1, parts):
-        peer = place(dz=d)
-        to_back.append(copy(6 + parts + d, back.at[peer[2]], returned.at[vz], peer))
-        to_back[-1].start()
-    returned[vz] = back[vz]
-    for each in to_back:
+    solve(factors, columns.at[1], back.at[1], 1, count)
+    back_1 = spread_out(1, first_back, back, returned)
+    sections((west, east), (0, 1, 2))
+    for each in back_0 + back_1:
         each.wait_recv()
-    for each in to_tables + to_edges + to_faces + to_columns + to_back:
+    for each in to_tables + to_edges + to_faces + out_0 + out_1 + back_0 + back_1:
         each.wait_send()
 
 
@@ -507,15 +595,18 @@
     flips = orientation.reshape(4, LANES)
     couples = coupling.reshape(4, levels * parts, 4, LANES)
     damp = damping.reshape(4, LANES)
-    copies = 6 + 2 * parts
+    copies = 8 + 4 * (parts - 1)
+    tiles = (levels + 2 + 3) // 4
     trace = pltpu.VMEM((FIELDS, levels, 4, LANES), jnp.float32)
-    column = pltpu.VMEM((parts, levels + 2, 4, LANES), jnp.float32)
+    column = pltpu.VMEM((2, parts, tiles, ROWS, LANES), jnp.float32)
     section, returned = pl.pallas_call(
         functools.partial(whole_kernel, sizes),
-        out_shape=(f32(FIELDS, levels, 16, LANES), f32(parts, levels + 2, 4, LANES)),
-        in_specs=[SM, SM] + [VM] * 7,
+        out_shape=(f32(FIELDS, levels, 16, LANES), f32(2, parts, tiles, ROWS, LANES)),
+        in_specs=[SM, SM, ANY, VM, VM, VM, ANY, VM, VM],
         out_specs=(VM, VM),
         scratch_shapes=[
+            pltpu.VMEM((FIELDS, levels, 16, LANES), jnp.float32),
+            pltpu.VMEM((4, levels * parts, 4, LANES), jnp.float32),
             pltpu.VMEM((4, 4, LANES), jnp.int32),
             trace,
             trace,
@@ -530,6 +621,7 @@
             column,
             pltpu.SemaphoreType.DMA((copies,)),
             pltpu.SemaphoreType.DMA((copies,)),
+            pltpu.SemaphoreType.DMA((2,)),
         ],
         compiler_params=pltpu.CompilerParams(collective_id=0, has_side_effects=True),
         name="exchange",

time: 57 us -> 53.7 us (0.942)
  Pallas kernels: 56.8 us -> 53.5 us
    pallas_call x1, Pallas kernels: 54.6 us -> 51.3 us  [per_device(): pl.pallas_call(functools.partial(whole_kernel, sizes), out_shape=(f32(FIE...]
where the time goes in v3:
time: 53.7 us; the launch traced here: 53.5 us
  Pallas kernels  53.5 us (100%)
    pallas_call x1, Pallas kernels, per_device(): pl.pallas_call(functools.partial(whole_kernel, sizes), out_shape=(f32(FIE...  51.3 us
    pallas_call x1, Pallas kernels, per_device(): pl.pallas_call(finish, out_shape=f32(FIELDS, levels, 16, LANES), in_specs...  2.15 us

profile of v3, /device:TPU:1, one launch (start us, length us, event | category | flops | bytes accessed | tf_op | source)
XLA Modules:
  0.0 53.5 jit_solution(13107901577277940331)
XLA Ops:
  0.0 51.3 %exchange.1 = (f32[5,20,16,128]{3,2,1,0:T(8,128)}, f32[2,4,6,8,128]{4,3,2,1,0:T(8,128)}) custom-call(f32[5,5]{1,0:T(8,128)} %first.1, f32[5,5]{1,0:T(8,128)} %second.1, f32[5,20,16,128]{3,2,1,0:T(8,128)} %bitcast.9, f32[16,128]{1,0:T(8,128)} %bitcast.11, s32[4,128]{1,0:T(4,128)} %bitcast.12, s32[4,128]{1,0:T(4,128)} %bitcast.13, f32[4,80,4,128]{3,2,1,0:T(4,128)} %bitcast.10, ...), custom_call_target="tpu_custom_call" | custom-call | tf_op jit(solution)/shard_map/exchange/pallas_call | solution.py:602
  51.4 2.2 %finish.1 = f32[5,20,16,128]{3,2,1,0:T(8,128)} custom-call(f32[5,20,16,128]{3,2,1,0:T(8,128)} %get-tuple-element.7.section, f32[2,4,6,8,128]{4,3,2,1,0:T(8,128)} %get-tuple-element.8.returned), custom_call_target="tpu_custom_call" | custom-call | tf_op jit(solution)/shard_map/finish/pallas_call | solution.py:639

commit v4 on v3

--- a/solution.py
+++ b/solution.py
@@ -171,7 +171,6 @@
     state, scale, first, second, faces, flips, sides, before, after, weights, section, targets
 ):
     levels = state.shape[1]
-    row, lane = rows_of(), lanes_of()
     node = halves(
         node_rows(
             pltpu.roll(spread(faces[2:3]), LANES - 1, 1),
@@ -179,8 +178,8 @@
         ),
         node_rows(pltpu.roll(spread(faces[3:4]), 1, 1), pltpu.roll(spread(flips[3:4]), 1, 1)),
     )
-    edge = edge_values(before, after, faces, flips)
-    at_edge = ((row < 4) & (lane == 0)) | ((row >= 4) & (lane == LANES - 1))
+    edge = None if before is None else edge_values(before, after, faces, flips)
+    at_edge = edge_mask()
     place = side_rows()
 
     def at(count, carry):
@@ -194,8 +193,10 @@
             swapped = [pltpu.roll(tile, 4, 0) for tile in tiles]
             chosen = take_nodes(tiles[0], tiles[1], node)
             across = halves(pltpu.roll(chosen, 1, 1), pltpu.roll(chosen, LANES - 1, 1))
-            shift = lax.rem(2 * LANES - number, LANES)
-            across = jnp.where(at_edge, pltpu.roll(edge, shift, 1), across)
+            if edge is None:
+                across = jnp.where(at_edge, 0.0, across)
+            else:
+                across = jnp.where(at_edge, edge_level(edge, number), across)
             if sides is not None:
                 beside = pair(sides[0][field, count], sides[1][field, count])
             for t in range(2):
@@ -231,6 +232,37 @@
     lax.fori_loop(0, levels, at, 0)
 
 
+def edge_mask():
+    row, lane = rows_of(), lanes_of()
+    return ((row < 4) & (lane == 0)) | ((row >= 4) & (lane == LANES - 1))
+
+
+def edge_level(edge, number):
+    return pltpu.roll(edge, lax.rem(2 * LANES - number, LANES), 1)
+
+
+def add_edges(scale, second, faces, flips, before, after, weights, section, targets):
+    levels = section.shape[1]
+    edge = edge_values(before, after, faces, flips)
+    at_edge = edge_mask()
+
+    def at(count, carry):
+        across = [
+            jnp.where(at_edge, edge_level(edge, g * levels + count), 0.0) for g in range(FIELDS)
+        ]
+        for field in targets:
+            total = second[field, 0] * across[0]
+            for other in range(1, FIELDS):
+                total += second[field, other] * across[other]
+            for t in range(2):
+                span = slice(t * ROWS, (t + 1) * ROWS)
+                change = weights[19 + t] * across[field] - weights[17 + t] * total
+                section[field, count, span] += step_size * scale[span] * change
+        return carry
+
+    lax.fori_loop(0, levels, at, 0, unroll=2)
+
+
 def side_rows():
     row = rows_of()
     left = row % 4 < 2
@@ -277,8 +309,15 @@
     return total
 
 
-def scattered(tile, m):
-    return take_rows(tile, 2 * m + (rows_of() % 4) // 2)
+def put_tile(message, p, tile):
+    for half in range(2):
+        if 2 * p + half < message.shape[0]:
+            message[2 * p + half] = tile[4 * half : 4 * half + 4]
+
+
+def scattered(message, place):
+    tile = message[place // 2]
+    return take_rows(pair(tile, tile), 2 * (place % 2) + (rows_of() % 4) // 2)
 
 
 def column_message(section, message, part):
@@ -298,9 +337,8 @@
         entries += [None] * (-len(entries) % 4)
         for p in range(len(entries) // 4):
             for side in range(2):
-                message[2 * t + side, p] = gathered(
-                    entries[4 * p : 4 * p + 4], [4 * side] * 4, part
-                )
+                tile = gathered(entries[4 * p : 4 * p + 4], [4 * side] * 4, part)
+                put_tile(message.at[2 * t + side], p, tile)
 
 
 def pair(low, high):
@@ -342,7 +380,7 @@
     half = levels // 2
 
     def entry_of(d, place):
-        return scattered(columns[d, place // 4], place % 4)
+        return scattered(columns.at[d], place)
 
     def source(level):
         d, place = level // count, level % count
@@ -384,7 +422,7 @@
                 low = level < half
                 entries.append((found[level] if low else found[levels - 1 - level]) if inside else None)
                 base.append(0 if low else 4)
-            message[d, p] = gathered(entries, base, part)
+            put_tile(message.at[d], p, gathered(entries, base, part))
 
 
 def finish(section, returned, updated):
@@ -395,12 +433,11 @@
         span = slice(t * ROWS, (t + 1) * ROWS)
 
         def level(place):
-            p, m = place // 4, place % 4
             both = [
                 jnp.where(
                     inner,
-                    scattered(returned[0, 2 * t + side, p], m),
-                    scattered(returned[1, 2 * t + side, p], m),
+                    scattered(returned.at[0, 2 * t + side], place),
+                    scattered(returned.at[1, 2 * t + side], place),
                 )
                 for side in range(2)
             ]
@@ -487,23 +524,39 @@
     load_coupling = pltpu.make_async_copy(coupling_in, coupling, load_sem.at[1])
     load_state.start()
     load_coupling.start()
+
+    def sections(sides, edge_pair, targets):
+        make_section(
+            state,
+            scale,
+            first,
+            second,
+            faces[...],
+            flips[...],
+            sides,
+            edge_pair[0],
+            edge_pair[1],
+            weights,
+            section,
+            targets,
+        )
+
+    load_state.wait()
+    pack_edges(state, edges)
     pl.semaphore_wait(barrier, len(partners))
+    to_edges = [
+        copy(4, edges.at[0], after, place(dx=-1)),
+        copy(5, edges.at[1], before, place(dx=1)),
+    ]
     to_tables = [
         copy(0, faces, tables.at[0], place(dy=-1)),
         copy(1, flips, tables.at[1], place(dy=-1)),
         copy(2, faces, tables.at[2], place(dy=1)),
         copy(3, flips, tables.at[3], place(dy=1)),
     ]
-    for each in to_tables:
+    for each in to_edges + to_tables:
         each.start()
-    load_state.wait()
-    pack_edges(state, edges)
-    to_edges = [
-        copy(4, edges.at[0], after, place(dx=-1)),
-        copy(5, edges.at[1], before, place(dx=1)),
-    ]
-    for each in to_edges:
-        each.start()
+    sections(None, (None, None), (3, 4))
     for each in to_tables:
         each.wait_recv()
     pack_faces(
@@ -520,24 +573,6 @@
     ]
     for each in to_faces:
         each.start()
-    for each in to_edges:
-        each.wait_recv()
-
-    def sections(sides, targets):
-        make_section(
-            state,
-            scale,
-            first,
-            second,
-            faces[...],
-            flips[...],
-            sides,
-            before[...],
-            after[...],
-            weights,
-            section,
-            targets,
-        )
 
     def spread_out(part, base, source, target):
         sent = []
@@ -551,7 +586,11 @@
 
     first_out, first_back = 8, 8 + 2 * (parts - 1)
     count = state.shape[1]
-    sections(None, (3, 4))
+    for each in to_edges:
+        each.wait_recv()
+    add_edges(
+        scale, second, faces[...], flips[...], before[...], after[...], weights, section, (3, 4)
+    )
     column_message(section, message.at[0], 0)
     out_0 = spread_out(0, first_out, message, columns)
     for each in to_faces:
@@ -569,7 +608,7 @@
         each.wait_recv()
     solve(factors, columns.at[1], back.at[1], 1, count)
     back_1 = spread_out(1, first_back, back, returned)
-    sections((west, east), (0, 1, 2))
+    sections((west, east), (before[...], after[...]), (0, 1, 2))
     for each in back_0 + back_1:
         each.wait_recv()
     for each in to_tables + to_edges + to_faces + out_0 + out_1 + back_0 + back_1:
@@ -596,12 +635,12 @@
     couples = coupling.reshape(4, levels * parts, 4, LANES)
     damp = damping.reshape(4, LANES)
     copies = 8 + 4 * (parts - 1)
-    tiles = (levels + 2 + 3) // 4
+    tiles = (levels + 3) // 2
     trace = pltpu.VMEM((FIELDS, levels, 4, LANES), jnp.float32)
-    column = pltpu.VMEM((2, parts, tiles, ROWS, LANES), jnp.float32)
+    column = pltpu.VMEM((2, parts, tiles, 4, LANES), jnp.float32)
     section, returned = pl.pallas_call(
         functools.partial(whole_kernel, sizes),
-        out_shape=(f32(FIELDS, levels, 16, LANES), f32(2, parts, tiles, ROWS, LANES)),
+        out_shape=(f32(FIELDS, levels, 16, LANES), f32(2, parts, tiles, 4, LANES)),
         in_specs=[SM, SM, ANY, VM, VM, VM, ANY, VM, VM],
         out_specs=(VM, VM),
         scratch_shapes=[

time: 53.7 us -> 51.6 us (0.961)
  the two profiles are of different devices: /device:TPU:1 before, /device:TPU:43 now
where the time goes in v4:
time: 51.6 us; the launch traced here: 51.4 us
  Pallas kernels  51.4 us (100%)
    pallas_call x1, Pallas kernels, per_device(): pl.pallas_call(functools.partial(whole_kernel, sizes), out_shape=(f32(FIE...  49.3 us
    pallas_call x1, Pallas kernels, per_device(): pl.pallas_call(finish, out_shape=f32(FIELDS, levels, 16, LANES), in_specs...  2.16 us

profile of v4, /device:TPU:43, one launch (start us, length us, event | category | flops | bytes accessed | tf_op | source)
XLA Modules:
  0.0 51.4 jit_solution(10736794429401166266)
XLA Ops:
  0.0 49.3 %exchange.1 = (f32[5,20,16,128]{3,2,1,0:T(8,128)}, f32[2,4,11,4,128]{4,3,2,1,0:T(4,128)}) custom-call(f32[5,5]{1,0:T(8,128)} %first.1, f32[5,5]{1,0:T(8,128)} %second.1, f32[5,20,16,128]{3,2,1,0:T(8,128)} %bitcast.9, f32[16,128]{1,0:T(8,128)} %bitcast.11, s32[4,128]{1,0:T(4,128)} %bitcast.12, s32[4,128]{1,0:T(4,128)} %bitcast.13, ...), custom_call_target="tpu_custom_call" | custom-call | tf_op jit(solution)/shard_map/exchange/pallas_call | solution.py:641
  49.3 2.2 %finish.1 = f32[5,20,16,128]{3,2,1,0:T(8,128)} custom-call(f32[5,20,16,128]{3,2,1,0:T(8,128)} %get-tuple-element.7.section, f32[2,4,11,4,128]{4,3,2,1,0:T(4,128)} %get-tuple-element.8.returned), custom_call_target="tpu_custom_call" | custom-call | tf_op jit(solution)/shard_map/finish/pallas_call | solution.py:678

commit v5 on v4

--- a/solution.py
+++ b/solution.py
@@ -320,8 +320,9 @@
     return take_rows(pair(tile, tile), 2 * (place % 2) + (rows_of() % 4) // 2)
 
 
-def column_message(section, message, part):
+def column_message(section, message, part, only_edges=False):
     levels = section.shape[1]
+    lane = lanes_of()
     for t in range(2):
         span = slice(t * ROWS, (t + 1) * ROWS)
         warm = [section[4, count, span] for count in range(levels)]
@@ -335,10 +336,30 @@
             entries.append(total)
         entries += [warm[0], warm[levels - 1]]
         entries += [None] * (-len(entries) % 4)
-        for p in range(len(entries) // 4):
-            for side in range(2):
+        for side in range(2):
+            packed = None
+            for p in range(len(entries) // 4):
                 tile = gathered(entries[4 * p : 4 * p + 4], [4 * side] * 4, part)
-                put_tile(message.at[2 * t + side], p, tile)
+                if only_edges:
+                    moved = pltpu.roll(tile, p + t, 1) if p + t else tile
+                    packed = moved if p == 0 else jnp.where(lane == p, moved, packed)
+                else:
+                    put_tile(message.at[2 * t + side], p, tile)
+            if only_edges:
+                message[2 * t + side] = packed
+
+
+def replace_edges(columns, patches, j):
+    lane = lanes_of((4, LANES))
+    target = (j // 2) * (LANES - 1)
+    for d in range(columns.shape[0]):
+        for p in range((columns.shape[1] + 1) // 2):
+            moved = pltpu.roll(patches[d], lax.rem(target + LANES - p, LANES), 1)
+            for half in range(2):
+                if 2 * p + half < columns.shape[1]:
+                    columns[d, 2 * p + half] = jnp.where(
+                        lane == target, moved[4 * half : 4 * half + 4], columns[d, 2 * p + half]
+                    )
 
 
 def pair(low, high):
@@ -490,6 +511,8 @@
     message,
     columns,
     back,
+    patch,
+    patches,
     send_sem,
     recv_sem,
     load_sem,
@@ -556,7 +579,21 @@
     ]
     for each in to_edges + to_tables:
         each.start()
+    def spread_out(part, base, source, target):
+        sent = []
+        for d in range(1, parts):
+            peer = place(dz=d)
+            number = base + part * (parts - 1) + d - 1
+            sent.append(copy(number, source.at[part, peer[2]], target.at[part, vz], peer))
+            sent[-1].start()
+        target[part, vz] = source[part, vz]
+        return sent
+
+    first_out, first_back = 8, 8 + 2 * (parts - 1)
+    count = state.shape[1]
     sections(None, (None, None), (3, 4))
+    column_message(section, message.at[0], 0)
+    out_0 = spread_out(0, first_out, message, columns)
     for each in to_tables:
         each.wait_recv()
     pack_faces(
@@ -573,35 +610,29 @@
     ]
     for each in to_faces:
         each.start()
-
-    def spread_out(part, base, source, target):
-        sent = []
-        for d in range(1, parts):
-            peer = place(dz=d)
-            number = base + part * (parts - 1) + d - 1
-            sent.append(copy(number, source.at[part, peer[2]], target.at[part, vz], peer))
-            sent[-1].start()
-        target[part, vz] = source[part, vz]
-        return sent
-
-    first_out, first_back = 8, 8 + 2 * (parts - 1)
-    count = state.shape[1]
+    load_coupling.wait()
+    factor(coupling, damping, factors)
     for each in to_edges:
         each.wait_recv()
     add_edges(
         scale, second, faces[...], flips[...], before[...], after[...], weights, section, (3, 4)
     )
-    column_message(section, message.at[0], 0)
-    out_0 = spread_out(0, first_out, message, columns)
+    column_message(section, patch, 0, only_edges=True)
+    to_patches = []
+    for d in range(1, parts):
+        peer = place(dz=d)
+        number = 8 + 4 * (parts - 1) + d - 1
+        to_patches.append(copy(number, patch.at[peer[2]], patches.at[vz], peer))
+        to_patches[-1].start()
+    patches[vz] = patch[vz]
     for each in to_faces:
         each.wait_recv()
     add_sides(scale, first, (west, east), weights, section, (3, 4))
     column_message(section, message.at[1], 1)
     out_1 = spread_out(1, first_out, message, columns)
-    load_coupling.wait()
-    factor(coupling, damping, factors)
-    for each in out_0:
+    for each in out_0 + to_patches:
         each.wait_recv()
+    replace_edges(columns.at[0], patches, vz)
     solve(factors, columns.at[0], back.at[0], 0, count)
     back_0 = spread_out(0, first_back, back, returned)
     for each in out_1:
@@ -611,7 +642,8 @@
     sections((west, east), (before[...], after[...]), (0, 1, 2))
     for each in back_0 + back_1:
         each.wait_recv()
-    for each in to_tables + to_edges + to_faces + out_0 + out_1 + back_0 + back_1:
+    sent = to_tables + to_edges + to_faces + to_patches + out_0 + out_1 + back_0 + back_1
+    for each in sent:
         each.wait_send()
 
 
@@ -634,7 +666,8 @@
     flips = orientation.reshape(4, LANES)
     couples = coupling.reshape(4, levels * parts, 4, LANES)
     damp = damping.reshape(4, LANES)
-    copies = 8 + 4 * (parts - 1)
+    copies = 8 + 5 * (parts - 1)
+    lanes_out = pltpu.VMEM((parts, ROWS, LANES), jnp.float32)
     tiles = (levels + 3) // 2
     trace = pltpu.VMEM((FIELDS, levels, 4, LANES), jnp.float32)
     column = pltpu.VMEM((2, parts, tiles, 4, LANES), jnp.float32)
@@ -658,6 +691,8 @@
             column,
             column,
             column,
+            lanes_out,
+            lanes_out,
             pltpu.SemaphoreType.DMA((copies,)),
             pltpu.SemaphoreType.DMA((copies,)),
             pltpu.SemaphoreType.DMA((2,)),

time: 51.6 us -> 50.3 us (0.975)
  the two profiles are of different devices: /device:TPU:43 before, /device:TPU:41 now
where the time goes in v5:
time: 50.3 us; the launch traced here: 50.1 us
  Pallas kernels  50.1 us (100%)
    pallas_call x1, Pallas kernels, per_device(): pl.pallas_call(functools.partial(whole_kernel, sizes), out_shape=(f32(FIE...  48 us
    pallas_call x1, Pallas kernels, per_device(): pl.pallas_call(finish, out_shape=f32(FIELDS, levels, 16, LANES), in_specs...  2.16 us

profile of v5, /device:TPU:41, one launch (start us, length us, event | category | flops | bytes accessed | tf_op | source)
XLA Modules:
  0.0 50.1 jit_solution(8187926571285665770)
XLA Ops:
  0.0 48.0 %exchange.1 = (f32[5,20,16,128]{3,2,1,0:T(8,128)}, f32[2,4,11,4,128]{4,3,2,1,0:T(4,128)}) custom-call(f32[5,5]{1,0:T(8,128)} %first.1, f32[5,5]{1,0:T(8,128)} %second.1, f32[5,20,16,128]{3,2,1,0:T(8,128)} %bitcast.9, f32[16,128]{1,0:T(8,128)} %bitcast.11, s32[4,128]{1,0:T(4,128)} %bitcast.12, s32[4,128]{1,0:T(4,128)} %bitcast.13, ...), custom_call_target="tpu_custom_call" | custom-call | tf_op jit(solution)/shard_map/exchange/pallas_call | solution.py:674
  48.0 2.2 %finish.1 = f32[5,20,16,128]{3,2,1,0:T(8,128)} custom-call(f32[5,20,16,128]{3,2,1,0:T(8,128)} %get-tuple-element.7.section, f32[2,4,11,4,128]{4,3,2,1,0:T(4,128)} %get-tuple-element.8.returned), custom_call_target="tpu_custom_call" | custom-call | tf_op jit(solution)/shard_map/finish/pallas_call | solution.py:713

commit v6 on v5

--- a/solution.py
+++ b/solution.py
@@ -122,7 +122,7 @@
             south_message[field, count] = chosen[4:8]
         return carry
 
-    lax.fori_loop(0, levels, at, 0, unroll=2)
+    lax.fori_loop(0, levels, at, 0, unroll=4)
 
 
 def pack_edges(state, edges):
@@ -144,7 +144,7 @@
                 held[2 + tile] = jnp.where(at_last, moved, held[2 + tile])
         return tuple(held)
 
-    held = lax.fori_loop(0, levels, at, (zero,) * 4)
+    held = lax.fori_loop(0, levels, at, (zero,) * 4, unroll=5)
     for tile in range(2):
         edges[0, tile * ROWS : (tile + 1) * ROWS] = held[tile]
         edges[1, tile * ROWS : (tile + 1) * ROWS] = held[2 + tile]
@@ -229,7 +229,7 @@
                 )
         return carry
 
-    lax.fori_loop(0, levels, at, 0)
+    lax.fori_loop(0, levels, at, 0, unroll=4)
 
 
 def edge_mask():
@@ -260,7 +260,7 @@
                 section[field, count, span] += step_size * scale[span] * change
         return carry
 
-    lax.fori_loop(0, levels, at, 0, unroll=2)
+    lax.fori_loop(0, levels, at, 0, unroll=4)
 
 
 def side_rows():
@@ -286,7 +286,7 @@
                 section[field, count, span] += step_size * scale[span] * total
         return carry
 
-    lax.fori_loop(0, levels, at, 0, unroll=2)
+    lax.fori_loop(0, levels, at, 0, unroll=4)
 
 
 def point_pair(part):

time: 50.3 us -> 51.8 us (1.030)
  the two profiles are of different devices: /device:TPU:41 before, /device:TPU:33 now
where the time goes in v6:
time: 51.8 us; the launch traced here: 51.6 us
  Pallas kernels  51.6 us (100%)
    pallas_call x1, Pallas kernels, per_device(): pl.pallas_call(functools.partial(whole_kernel, sizes), out_shape=(f32(FIE...  49.4 us
    pallas_call x1, Pallas kernels, per_device(): pl.pallas_call(finish, out_shape=f32(FIELDS, levels, 16, LANES), in_specs...  2.16 us

profile of v6, /device:TPU:33, one launch (start us, length us, event | category | flops | bytes accessed | tf_op | source)
XLA Modules:
  0.0 51.6 jit_solution(10695311423606034962)
XLA Ops:
  0.0 49.4 %exchange.1 = (f32[5,20,16,128]{3,2,1,0:T(8,128)}, f32[2,4,11,4,128]{4,3,2,1,0:T(4,128)}) custom-call(f32[5,5]{1,0:T(8,128)} %first.1, f32[5,5]{1,0:T(8,128)} %second.1, f32[5,20,16,128]{3,2,1,0:T(8,128)} %bitcast.9, f32[16,128]{1,0:T(8,128)} %bitcast.11, s32[4,128]{1,0:T(4,128)} %bitcast.12, s32[4,128]{1,0:T(4,128)} %bitcast.13, ...), custom_call_target="tpu_custom_call" | custom-call | tf_op jit(solution)/shard_map/exchange/pallas_call | solution.py:674
  49.4 2.2 %finish.1 = f32[5,20,16,128]{3,2,1,0:T(8,128)} custom-call(f32[5,20,16,128]{3,2,1,0:T(8,128)} %get-tuple-element.7.section, f32[2,4,11,4,128]{4,3,2,1,0:T(4,128)} %get-tuple-element.8.returned), custom_call_target="tpu_custom_call" | custom-call | tf_op jit(solution)/shard_map/finish/pallas_call | solution.py:713

commit v7 on v5

--- a/solution.py
+++ b/solution.py
@@ -495,8 +495,9 @@
     coupling_in,
     damping,
     weights,
+    section_out,
+    returned,
     section,
-    returned,
     state,
     coupling,
     tables,
@@ -640,11 +641,14 @@
     solve(factors, columns.at[1], back.at[1], 1, count)
     back_1 = spread_out(1, first_back, back, returned)
     sections((west, east), (before[...], after[...]), (0, 1, 2))
+    store_section = pltpu.make_async_copy(section, section_out, load_sem.at[2])
+    store_section.start()
     for each in back_0 + back_1:
         each.wait_recv()
     sent = to_tables + to_edges + to_faces + to_patches + out_0 + out_1 + back_0 + back_1
     for each in sent:
         each.wait_send()
+    store_section.wait()
 
 
 def per_device(
@@ -675,8 +679,9 @@
         functools.partial(whole_kernel, sizes),
         out_shape=(f32(FIELDS, levels, 16, LANES), f32(2, parts, tiles, 4, LANES)),
         in_specs=[SM, SM, ANY, VM, VM, VM, ANY, VM, VM],
-        out_specs=(VM, VM),
+        out_specs=(ANY, VM),
         scratch_shapes=[
+            pltpu.VMEM((FIELDS, levels, 16, LANES), jnp.float32),
             pltpu.VMEM((FIELDS, levels, 16, LANES), jnp.float32),
             pltpu.VMEM((4, levels * parts, 4, LANES), jnp.float32),
             pltpu.VMEM((4, 4, LANES), jnp.int32),
@@ -695,7 +700,7 @@
             lanes_out,
             pltpu.SemaphoreType.DMA((copies,)),
             pltpu.SemaphoreType.DMA((copies,)),
-            pltpu.SemaphoreType.DMA((2,)),
+            pltpu.SemaphoreType.DMA((3,)),
         ],
         compiler_params=pltpu.CompilerParams(collective_id=0, has_side_effects=True),
         name="exchange",

time: 50.3 us -> 50 us (level)
  no operation moved by 1% of the time
where the time goes in v7:
time: 50 us; the launch traced here: 49.8 us
  Pallas kernels  49.8 us (100%)
    pallas_call x1, Pallas kernels, per_device(): pl.pallas_call(functools.partial(whole_kernel, sizes), out_shape=(f32(FIE...  47.6 us
    pallas_call x1, Pallas kernels, per_device(): pl.pallas_call(finish, out_shape=f32(FIELDS, levels, 16, LANES), in_specs...  2.16 us

profile of v7, /device:TPU:41, one launch (start us, length us, event | category | flops | bytes accessed | tf_op | source)
XLA Modules:
  0.0 49.8 jit_solution(10676938405283382738)
XLA Ops:
  0.0 47.6 %exchange.1 = (f32[5,20,16,128]{3,2,1,0:T(8,128)}, f32[2,4,11,4,128]{4,3,2,1,0:T(4,128)}) custom-call(f32[5,5]{1,0:T(8,128)} %first.1, f32[5,5]{1,0:T(8,128)} %second.1, f32[5,20,16,128]{3,2,1,0:T(8,128)} %bitcast.9, f32[16,128]{1,0:T(8,128)} %bitcast.11, s32[4,128]{1,0:T(4,128)} %bitcast.12, s32[4,128]{1,0:T(4,128)} %bitcast.13, ...), custom_call_target="tpu_custom_call" | custom-call | tf_op jit(solution)/shard_map/exchange/pallas_call | solution.py:678
  47.6 2.2 %finish.1 = f32[5,20,16,128]{3,2,1,0:T(8,128)} custom-call(f32[5,20,16,128]{3,2,1,0:T(8,128)} %get-tuple-element.7.section, f32[2,4,11,4,128]{4,3,2,1,0:T(4,128)} %get-tuple-element.8.returned), custom_call_target="tpu_custom_call" | custom-call | tf_op jit(solution)/shard_map/finish/pallas_call | solution.py:718

commit v8 on v7

--- a/solution.py
+++ b/solution.py
@@ -144,7 +144,7 @@
                 held[2 + tile] = jnp.where(at_last, moved, held[2 + tile])
         return tuple(held)
 
-    held = lax.fori_loop(0, levels, at, (zero,) * 4)
+    held = lax.fori_loop(0, levels, at, (zero,) * 4, unroll=4)
     for tile in range(2):
         edges[0, tile * ROWS : (tile + 1) * ROWS] = held[tile]
         edges[1, tile * ROWS : (tile + 1) * ROWS] = held[2 + tile]

time: 50 us -> 51 us (1.020)
  the two profiles are of different devices: /device:TPU:41 before, /device:TPU:53 now
where the time goes in v8:
time: 51 us; the launch traced here: 50.8 us
  Pallas kernels  50.8 us (100%)
    pallas_call x1, Pallas kernels, per_device(): pl.pallas_call(functools.partial(whole_kernel, sizes), out_shape=(f32(FIE...  48.6 us
    pallas_call x1, Pallas kernels, per_device(): pl.pallas_call(finish, out_shape=f32(FIELDS, levels, 16, LANES), in_specs...  2.16 us

profile of v8, /device:TPU:53, one launch (start us, length us, event | category | flops | bytes accessed | tf_op | source)
XLA Modules:
  0.0 50.8 jit_solution(12101353767825066310)
XLA Ops:
  0.0 48.6 %exchange.1 = (f32[5,20,16,128]{3,2,1,0:T(8,128)}, f32[2,4,11,4,128]{4,3,2,1,0:T(4,128)}) custom-call(f32[5,5]{1,0:T(8,128)} %first.1, f32[5,5]{1,0:T(8,128)} %second.1, f32[5,20,16,128]{3,2,1,0:T(8,128)} %bitcast.9, f32[16,128]{1,0:T(8,128)} %bitcast.11, s32[4,128]{1,0:T(4,128)} %bitcast.12, s32[4,128]{1,0:T(4,128)} %bitcast.13, ...), custom_call_target="tpu_custom_call" | custom-call | tf_op jit(solution)/shard_map/exchange/pallas_call | solution.py:678
  48.6 2.2 %finish.1 = f32[5,20,16,128]{3,2,1,0:T(8,128)} custom-call(f32[5,20,16,128]{3,2,1,0:T(8,128)} %get-tuple-element.7.section, f32[2,4,11,4,128]{4,3,2,1,0:T(4,128)} %get-tuple-element.8.returned), custom_call_target="tpu_custom_call" | custom-call | tf_op jit(solution)/shard_map/finish/pallas_call | solution.py:718
